TPU v7x, 512 devices: a whole 4x8x8 slice. The times are simulated.
512 devices in a mesh: row: 16 (over z_lo, x, core), col: 32 (over y, z_hi).
Axes of the slice: x: 4, y: 8, z: 8 (z_hi: 4, z_lo: 2; z = z_hi * 2 + z_lo), core: 2. Of those that a mesh axis runs over, the one named last changes fastest.
Arguments:
- amplitudes: bfloat16 [1, 8, 4096, 4096], P(None, None, 'row', 'col'), may hold values from -6 to 6
- factors: bfloat16 [1024, 8, 4096], P('col', None, 'row'), may hold values from -0.03125 to 0.03125
Outputs:
- residual: bfloat16 [1, 8, 4096, 4096], P(None, None, 'row', 'col')
All inputs are finite; a program needn't handle non-finite values.
Results may differ from a plain program's by a relative error of at most 0.0049.
Values may be sent and summed in bfloat16 or wider, within the bound.
No kernel may reach another device: no remote copies, remote signals or barrier semaphores. Data moves between devices by JAX's collectives and lax.ppermute only.
A program may use at most 64 MiB of HBM per device.

v0:
```python
import jax
import jax.numpy as jnp
from jax import lax
from jax.sharding import PartitionSpec as P


def broadcast(value, axis, source):
    kept = jnp.where(lax.axis_index(axis) == source, value, 0).astype(value.dtype)
    return lax.psum(kept, axis)


def body(amplitudes, factors):
    row_index = lax.axis_index("row")
    col_index = lax.axis_index("col")
    block_b = amplitudes.shape[3]
    row_factors = lax.all_gather(factors, "col", axis=0, tiled=True)
    offset = col_index % 2 * block_b
    own_piece = lax.dynamic_slice_in_dim(row_factors, offset, block_b, 2)
    col_factors = broadcast(own_piece, "row", col_index // 2)
    direct = jnp.einsum(
        "ijab,qjb->iqa", amplitudes, col_factors, preferred_element_type=jnp.float32
    )
    mirror = jnp.einsum(
        "ijxy,qjx->iqy", amplitudes, row_factors, preferred_element_type=jnp.float32
    )
    mirror_total = lax.psum(mirror, "row")
    pieces = []
    for parity in range(2):
        pieces.append(broadcast(mirror_total, "col", 2 * row_index + parity))
    mirror_rows = jnp.concatenate(pieces, axis=2)
    summand = 2.0 * direct
    total = lax.psum(summand, "col")
    total = total - mirror_rows
    fitted = total.astype(jnp.bfloat16)
    result = jnp.einsum("iqa,qjb->ijab", fitted, col_factors, preferred_element_type=jnp.float32)
    return result.astype(jnp.bfloat16)


def solution(mesh):
    placed = (P(None, None, "row", "col"), P("col", None, "row"))
    return jax.shard_map(
        body, mesh=mesh, in_specs=placed, out_specs=P(None, None, "row", "col"), check_vma=False
    )
```

profile of v0, /device:TPU:4, one launch (start us, length us, event | category | flops | bytes accessed | tf_op | source)
XLA Modules:
  0.0 724.4 jit_solution(13464338641774851621)
XLA Ops:
  6.5 0.0 copy-start
  6.5 0.0 all-gather.2.cloned.1.call-start
  6.5 1.6 copy.3
  8.2 0.0 all-gather.2.cloned.1.call-update
  8.2 0.0 all-reduce.7.cloned.1.call-start
  8.3 110.0 %all-gather.2.cloned.1.call-done = bf16[1024,8,256]{2,0,1:T(8,128)(2,1)} async-done(((bf16[32,8,256]{2,0,1:T(8,128)(2,1)}), bf16[1024,8,256]{2,0,1:T(8,128)(2,1)}) %all-gather.2.cloned.1.call-update) | async-done | bytes 4194320 | tf_op jit(solution)/shard_map/all_gather | solution.py:16
  118.2 0.0 copy-done
  118.2 4.2 convolution_bitcast_fusion.1
  122.5 0.0 all-reduce.7.cloned.1.call-update
  122.5 0.0 all-reduce.5.cloned.1.call-start
  122.6 3.4 dynamic-slice_select_fusion
  125.9 0.0 all-reduce.5.cloned.1.call-update
  126.0 0.0 all-reduce.9.cloned.1.call-start
  126.0 115.0 %all-reduce.7.cloned.1.call-done = f32[1,1024,128]{2,1,0:T(8,128)} async-done(((f32[1,1024,128]{2,1,0:T(8,128)}), f32[1,1024,128]{2,1,0:T(8,128)}) %all-reduce.7.cloned.1.call-update) | async-done | bytes 524304 | tf_op jit(solution)/shard_map/psum | solution.py:26
  241.1 2.1 broadcast_select_fusion.1
  243.1 135.2 %all-reduce.5.cloned.1.call-done = bf16[1024,8,128]{2,0,1:T(8,128)(2,1)} async-done(((bf16[1024,8,128]{2,0,1:T(8,128)(2,1)}), bf16[1024,8,128]{2,0,1:T(8,128)(2,1)}) %all-reduce.5.cloned.1.call-update) | async-done | bytes 2097168 | tf_op jit(solution)/shard_map/psum | solution.py:9
  378.3 3.3 fusion.1
  381.6 0.0 copy-start.1
  381.6 0.0 all-reduce.9.cloned.1.call-update
  381.6 332.9 %all-reduce.9.cloned.1.call-done = (f32[1,1024,256]{2,1,0:T(8,128)}, f32[1,1024,128]{2,1,0:T(8,128)}, f32[1,1024,128]{2,1,0:T(8,128)}) async-done(((f32[1,1024,256]{2,1,0:T(8,128)}, f32[1,1024,128]{2,1,0:T(8,128)}, f32[1,1024,128]{2,1,0:T(8,128)}), (f32[1,1024,256]{2,1,0:T(8,128)}, f32[1,1024,128]{2,1,0:T(8,128)}, f32[1,1024,128]{2,1,0:T(8,128)})) %all-reduce.9.cloned.1.call-update) | async-done | bytes 2097168 | tf_op jit(solution)/shard_map/psum | solution.py:32
  714.6 0.0 copy-done.1
  714.6 2.3 fusion.2
  716.8 1.0 copy.5
Async XLA Ops:
  6.5 111.7 %copy-start = (bf16[1,8,256,128]{3,2,1,0:T(8,128)(2,1)S(1)}, bf16[1,8,256,128]{3,2,1,0:T(8,128)(2,1)}, u32[]{:S(2)}) copy-start(bf16[1,8,256,128]{3,2,1,0:T(8,128)(2,1)} %param.2) | copy-start | bytes 1572868
  6.5 111.7 %all-gather.2.cloned.1.call-start = ((), (), s32[]{:S(2)}) async-start(), calls=%async_computation | async-start | bytes 4325376 | tf_op jit(solution)/shard_map/all_gather | solution.py:16
  8.2 232.8 %all-reduce.7.cloned.1.call-start = ((), (), s32[]{:S(2)}) async-start(), calls=%async_computation.2 | async-start | bytes 1048576 | tf_op jit(solution)/shard_map/psum | solution.py:26
  122.5 255.8 %all-reduce.5.cloned.1.call-start = ((), (), s32[]{:S(2)}) async-start(), calls=%async_computation.1 | async-start | bytes 4194304 | tf_op jit(solution)/shard_map/psum | solution.py:9
  126.0 588.6 %all-reduce.9.cloned.1.call-start = ((), (), s32[]{:S(2)}) async-start(), calls=%async_computation.3 | async-start | bytes 4194304 | tf_op jit(solution)/shard_map/psum | solution.py:32
  381.6 332.9 %copy-start.1 = (bf16[1024,8,128]{2,0,1:T(8,128)(2,1)S(1)}, bf16[1024,8,128]{2,0,1:T(8,128)(2,1)}, u32[]{:S(2)}) copy-start(bf16[1024,8,128]{2,0,1:T(8,128)(2,1)} %all-reduce.5.cloned.1.call-done) | copy-start | bytes 6291460
Sparse Core Ops, SparseCore 0:
  10.6 107.6 all-gather.1
  122.6 118.4 all-reduce.6
  244.3 134.0 all-reduce.4
  381.8 332.7 all-reduce.8
where the time goes:
time: 725 us; the launch traced here: 724 us
  waiting for transfers between devices  693 us (96%)
  between operations  13.2 us (2%)
  matrix products  9.81 us (1%)
    psum x1, waiting for transfers between devices, body(): total = lax.psum(summand, 'col')  333 us
    psum x1, waiting for transfers between devices, broadcast(): return lax.psum(kept, axis)  135 us
    psum x1, waiting for transfers between devices, body(): mirror_total = lax.psum(mirror, 'row')  115 us
    all_gather x1, waiting for transfers between devices, body(): row_factors = lax.all_gather(factors, 'col', axis=0, tiled=True)  110 us
  transfers between devices with their start and end apart: 4, of which 4 were waited for; matrix products, arithmetic and copies ran while one was open for 1% of the time, Pallas kernels for 0%

commit v1 on v0

v1 whole, which is shorter than its diff:
```python
import jax
import jax.numpy as jnp
from jax import lax
from jax.sharding import PartitionSpec as P

F32 = jnp.float32
BF16 = jnp.bfloat16


def body(amplitudes, factors):
    rows = lax.axis_size("row")
    cols = lax.axis_size("col")
    col_index = lax.axis_index("col")
    _, nj, block_a, block_b = amplitudes.shape
    block_q = factors.shape[0]
    aux = block_q * cols
    t = amplitudes[0]
    odd = lax.rem(col_index, 2)

    by_j = jnp.transpose(factors, (1, 0, 2))
    first, second = by_j[:, :, :block_b], by_j[:, :, block_b:]
    got = []
    for flip in range(2):
        piece = jnp.where(odd == flip, first, second)
        pairs = [
            (r * cols + c, (c // 2) * cols + 2 * r + ((c % 2) ^ flip))
            for r in range(rows)
            for c in range(cols)
        ]
        got.append(lax.ppermute(piece, ("row", "col"), pairs))
    low = jnp.where(odd == 0, got[0], got[1])
    high = jnp.where(odd == 0, got[1], got[0])
    own = jnp.concatenate([low, high], axis=1)

    half = block_b // 2
    x = t.reshape(nj, 2, 2, half, block_b)
    x = jnp.transpose(x, (0, 2, 1, 3, 4)).reshape(rows, 2 * half, block_b)
    x = lax.all_to_all(x, "row", 0, 0, tiled=True)
    x = x.reshape(cols, half, block_b)
    x = lax.all_to_all(x, "col", 0, 0, tiled=True)
    x = x.reshape(rows, 2 * half, block_b)
    x = lax.all_to_all(x, "row", 0, 0, tiled=True)
    x = x.reshape(nj, 2, 2, half, block_b)
    swapped = jnp.transpose(x, (0, 1, 3, 2, 4)).reshape(nj, block_b, block_a)

    gathered = lax.all_gather(own, "row", axis=1, tiled=True)

    direct = jnp.einsum("jab,jqb->qa", t, gathered, preferred_element_type=F32)
    mirror = jnp.einsum("jqs,jsa->qa", gathered, swapped, preferred_element_type=F32)
    partial = (2.0 * direct - mirror).astype(BF16)

    parts = partial.reshape(cols, block_q, block_a)
    parts = lax.all_to_all(parts, "col", 0, 0, tiled=True)
    shard = jnp.sum(parts.astype(F32), axis=0).astype(BF16)
    copies = jnp.broadcast_to(shard[None], (cols, block_q, block_a))
    fitted = lax.all_to_all(copies, "col", 0, 0, tiled=True).reshape(aux, block_a)

    result = jnp.einsum("qa,jqb->jab", fitted, gathered, preferred_element_type=F32)
    return result.astype(BF16)[None]


def solution(mesh):
    placed = (P(None, None, "row", "col"), P("col", None, "row"))
    return jax.shard_map(
        body, mesh=mesh, in_specs=placed, out_specs=P(None, None, "row", "col"), check_vma=False
    )
```

time: 725 us -> 159 us (0.22)
  the two profiles are of different devices: /device:TPU:4 before, /device:TPU:8 now
where the time goes in v1:
time: 159 us
  blocking collectives  124 us (78%)
  between operations  13.5 us (8%)
  starting transfers between devices  10.4 us (7%)
  local copies, waits for them, and re-layouts  3.95 us (2%)
  matrix products  3.95 us (2%)
  waiting for transfers between devices  2.26 us (1%)
    all_to_all x2, blocking collectives, body(): x = lax.all_to_all(x, 'row', 0, 0, tiled=True)  47.3 us
    all_to_all x1, blocking collectives, body(): x = lax.all_to_all(x, 'col', 0, 0, tiled=True)  28.7 us
    all_to_all x1, blocking collectives, body(): parts = lax.all_to_all(parts, 'col', 0, 0, tiled=True)  24.3 us
    all_to_all x1, blocking collectives, body(): lax.all_to_all(copies, 'col', 0, 0, tiled=True).reshape(aux, block_a)  23.7 us
    ppermute x2, starting transfers between devices, body(): got.append(lax.ppermute(piece, ('row', 'col'), pairs))  10.4 us
  transfers between devices with their start and end apart: 3, of which 1 were waited for; matrix products, arithmetic and copies ran while one was open for 1% of the time, Pallas kernels for 0%

profile of v1, /device:TPU:8, one launch (start us, length us, event | category | flops | bytes accessed | tf_op | source)
XLA Modules:
  0.0 158.8 jit_solution(7757580677726045489)
XLA Ops:
  6.5 0.0 all-gather.2.cloned.1.call-start
  6.5 0.9 copy.13
  7.5 3.3 %collective-permute-start = (bf16[8,32,128]{2,1,0:T(8,128)(2,1)S(1)}, bf16[8,32,128]{2,1,0:T(8,128)(2,1)S(1)}, u32[]{:S(2)}, u32[]{:S(2)}) collective-permute-start(bf16[8,32,128]{2,1,0:T(8,128)(2,1)S(1)} %get-tuple-element.7), channel_id=1, source_target_pairs={{0,0},{1,1},{2,32},{3,33},{4,64},{5,65},{6,96},{7,97},{8,128},{9,1... | collective-permute-start | bytes 196616 | tf_op jit(solution)/shard_map/ppermute | solution.py:30
  10.8 7.1 %collective-permute-start.1 = (bf16[8,32,128]{2,1,0:T(8,128)(2,1)S(1)}, bf16[8,32,128]{2,1,0:T(8,128)(2,1)S(1)}, u32[]{:S(2)}, u32[]{:S(2)}) collective-permute-start(bf16[8,32,128]{2,1,0:T(8,128)(2,1)S(1)} %get-tuple-element.8), channel_id=1, source_target_pairs={{0,1},{1,0},{2,33},{3,32},{4,65},{5,64},{6,97},{7,96},{8,129},{9,1... | collective-permute-start | bytes 196616 | tf_op jit(solution)/shard_map/ppermute | solution.py:30
  17.9 0.0 collective-permute-done
  17.9 2.2 %collective-permute-done.1 = bf16[8,32,128]{2,1,0:T(8,128)(2,1)S(1)} collective-permute-done((bf16[8,32,128]{2,1,0:T(8,128)(2,1)S(1)}, bf16[8,32,128]{2,1,0:T(8,128)(2,1)S(1)}, u32[]{:S(2)}, u32[]{:S(2)}) %collective-permute-start.1) | collective-permute-done | bytes 65568 | tf_op jit(solution)/shard_map/ppermute | solution.py:30
  20.1 0.7 pad_maximum_fusion
  20.8 0.0 all-gather.2.cloned.1.call-update
  20.8 1.1 copy.9
  21.9 33.6 %all_to_all.25 = bf16[16,128,128]{2,1,0:T(8,128)(2,1)S(1)} all-to-all(bf16[16,128,128]{2,1,0:T(8,128)(2,1)S(1)} %bitcast.41), channel_id=1, replica_groups=mesh['row'=16,'col'=32] {'row'}, dimensions={0} | all-to-all | bytes 1048576 | tf_op jit(solution)/shard_map/all_to_all | solution.py:38
  55.5 28.7 %all_to_all.26 = bf16[32,64,128]{2,1,0:T(8,128)(2,1)S(1)} all-to-all(bf16[32,64,128]{2,1,0:T(8,128)(2,1)S(1)} %bitcast.38), channel_id=1, replica_groups=mesh['row'=16,'col'=32] {'col'}, dimensions={0} | all-to-all | bytes 1048576 | tf_op jit(solution)/shard_map/all_to_all | solution.py:40
  84.2 13.7 %all_to_all.27 = bf16[16,128,128]{2,1,0:T(8,128)(2,1)S(1)} all-to-all(bf16[16,128,128]{2,1,0:T(8,128)(2,1)S(1)} %bitcast.39), channel_id=1, replica_groups=mesh['row'=16,'col'=32] {'row'}, dimensions={0} | all-to-all | bytes 1048576 | tf_op jit(solution)/shard_map/all_to_all | solution.py:42
  98.0 0.5 copy.10
  98.5 0.3 reshape.26
  98.9 0.0 copy-start.1
  98.9 0.0 all-gather.2.cloned.1.call-done
  98.9 0.0 copy-start
  98.9 2.4 %convolution_bitcast_fusion = f32[1024,256]{1,0:T(8,128)S(1)} fusion(bf16[8,1024,128]{2,1,0:T(8,128)(2,1)} %all-gather.2.cloned.1.call-done, bf16[8,128,256]{2,1,0:T(8,128)(2,1)S(1)} %reshape.26), kind=kOutput, calls=%fused_computation | convolution fusion | flops 536870912 | bytes 3670016 | tf_op jit(solution)/shard_map/jqs,jsa->qa/dot_general | solution.py:49
  101.4 0.0 copy-done.1
  101.4 0.0 copy-done
  101.4 0.8 fusion.2
  102.1 24.3 %all_to_all.28 = bf16[32,32,256]{2,1,0:T(8,128)(2,1)S(1)} all-to-all(bf16[32,32,256]{2,1,0:T(8,128)(2,1)S(1)} %bitcast.44), channel_id=1, replica_groups=mesh['row'=16,'col'=32] {'col'}, dimensions={0} | all-to-all | bytes 1048576 | tf_op jit(solution)/shard_map/all_to_all | solution.py:53
  126.4 0.1 reduce_sum.12
  126.5 0.1 broadcast_in_dim.4
  126.5 23.7 %all_to_all.29 = bf16[32,32,256]{2,1,0:T(8,128)(2,1)S(1)} all-to-all(bf16[32,32,256]{2,1,0:T(8,128)(2,1)S(1)} %broadcast_in_dim.4), channel_id=1, replica_groups=mesh['row'=16,'col'=32] {'col'}, dimensions={0} | all-to-all | bytes 1048576 | tf_op jit(solution)/shard_map/all_to_all | solution.py:56
  150.2 0.8 fusion.3
  151.0 1.0 copy.11
  (2 shorter events, 0.0 us)
Async XLA Ops:
  6.5 92.4 %all-gather.2.cloned.1.call-start = ((), (), s32[]{:S(2)}) async-start(), calls=%async_computation.5 | async-start | bytes 2228224 | tf_op jit(solution)/shard_map/all_gather | solution.py:46
  7.5 10.4 %collective-permute-start = (bf16[8,32,128]{2,1,0:T(8,128)(2,1)S(1)}, bf16[8,32,128]{2,1,0:T(8,128)(2,1)S(1)}, u32[]{:S(2)}, u32[]{:S(2)}) collective-permute-start(bf16[8,32,128]{2,1,0:T(8,128)(2,1)S(1)} %get-tuple-element.7), channel_id=1, source_target_pairs={{0,0},{1,1},{2,32},{3,33},{4,64},{5,65},{6,96},{7,97},{8,128},{9,1... | collective-permute-start | bytes 196616 | tf_op jit(solution)/shard_map/ppermute | solution.py:30
  10.8 9.3 %collective-permute-start.1 = (bf16[8,32,128]{2,1,0:T(8,128)(2,1)S(1)}, bf16[8,32,128]{2,1,0:T(8,128)(2,1)S(1)}, u32[]{:S(2)}, u32[]{:S(2)}) collective-permute-start(bf16[8,32,128]{2,1,0:T(8,128)(2,1)S(1)} %get-tuple-element.8), channel_id=1, source_target_pairs={{0,1},{1,0},{2,33},{3,32},{4,65},{5,64},{6,97},{7,96},{8,129},{9,1... | collective-permute-start | bytes 196616 | tf_op jit(solution)/shard_map/ppermute | solution.py:30
  98.9 2.5 %copy-start.1 = (bf16[1,8,256,128]{3,2,1,0:T(8,128)(2,1)S(1)}, bf16[1,8,256,128]{3,2,1,0:T(8,128)(2,1)}, u32[]{:S(2)}) copy-start(bf16[1,8,256,128]{3,2,1,0:T(8,128)(2,1)} %param.2) | copy-start | bytes 1572868
  98.9 2.5 %copy-start = (bf16[8,1024,128]{2,1,0:T(8,128)(2,1)S(1)}, bf16[8,1024,128]{2,1,0:T(8,128)(2,1)}, u32[]{:S(2)}) copy-start(bf16[8,1024,128]{2,1,0:T(8,128)(2,1)} %all-gather.2.cloned.1.call-done) | copy-start | bytes 6291460
Sparse Core Ops, SparseCore 0:
  20.9 64.4 all-gather.1

commit v2 on v1

v2 whole, which is shorter than its diff:
```python
import jax
import jax.numpy as jnp
from jax import lax
from jax.sharding import Mesh, PartitionSpec as P

F32 = jnp.float32
BF16 = jnp.bfloat16


def exchange(value, axes):
    return lax.all_to_all(value, axes, 0, 0, tiled=True)


def body(amplitudes, factors):
    cores = lax.axis_size("core")
    chips = lax.axis_size("chip")
    cols = lax.axis_size("col")
    rows = chips * cores
    _, nj, block_a, block_b = amplitudes.shape
    block_q = factors.shape[0]
    aux = block_q * cols
    half = block_b // 2
    few = block_q // 2
    t = amplitudes[0]

    x = jnp.transpose(t.reshape(nj, 2, 2, half, block_b), (0, 2, 1, 3, 4))
    x = x.reshape(rows, 2, half, block_b)
    y = jnp.transpose(factors.reshape(2, few, nj, 2, block_b), (2, 0, 3, 1, 4))
    y = y.reshape(rows, 2, few, block_b)
    both = jnp.concatenate([x, y], axis=2)
    both = exchange(both, ("chip", "core"))
    both = both.reshape(cols, half + few, block_b)
    both = exchange(both, "col")
    x, y = both[:, :half], both[:, half:]

    x = x.reshape(chips, 2 * 2 * half, block_b)
    y = jnp.broadcast_to(y.reshape(1, cols * few, block_b), (chips, cols * few, block_b))
    both = exchange(jnp.concatenate([x, y], axis=1), "chip")
    x, own = both[:, : 4 * half], both[:, 4 * half :]

    other = lax.ppermute(own, "core", [(k, (k + 1) % 2) for k in range(2)])
    x = jnp.transpose(x.reshape(nj, 2, 2, half, block_b), (1, 0, 2, 3, 4))
    x = exchange(x.reshape(2, nj * 2 * half, block_b), "core")
    x = x.reshape(2, nj, 2, half, block_b)
    swapped = jnp.transpose(x, (1, 0, 3, 2, 4)).reshape(nj, block_b, block_a)

    pieces = []
    for held in (own, other):
        direct = jnp.einsum("jab,jqb->qa", t, held, preferred_element_type=F32)
        mirror = jnp.einsum("jqs,jsa->qa", held, swapped, preferred_element_type=F32)
        pieces.append((2.0 * direct - mirror).astype(BF16))
    parts = jnp.concatenate(pieces, axis=0).reshape(cols, block_q, block_a)

    parts = exchange(parts, "col")
    shard = jnp.sum(parts.astype(F32), axis=0).astype(BF16)
    copies = jnp.broadcast_to(shard[None], (cols, block_q, block_a))
    fitted = exchange(copies, "col").reshape(2, aux // 2, block_a)

    result = jnp.einsum("qa,jqb->jab", fitted[0], own, preferred_element_type=F32)
    result = result + jnp.einsum("qa,jqb->jab", fitted[1], other, preferred_element_type=F32)
    return result.astype(BF16)[None]


def solution(mesh):
    rows, cols = mesh.devices.shape
    fine = Mesh(mesh.devices.reshape(rows // 2, 2, cols), ("chip", "core", "col"))
    row = ("chip", "core")
    placed = (P(None, None, row, "col"), P("col", None, row))
    return jax.shard_map(
        body, mesh=fine, in_specs=placed, out_specs=P(None, None, row, "col"), check_vma=False
    )
```

time: 159 us -> 145 us (0.912)
  between operations: 13.5 us -> 0.17 us
  starting transfers between devices: 10.4 us -> 1.91 us
  blocking collectives: 124 us -> 132 us
  local copies, waits for them, and re-layouts: 3.95 us -> 6.64 us
  waiting for transfers between devices: 2.26 us -> 0.01 us
    ppermute x2 -> x1, starting transfers between devices: 10.4 us -> 1.91 us  [body(): other = lax.ppermute(own, 'core', [(k, (k + 1) % 2) for k in range(2)])]
    all_to_all x5 -> x6, blocking collectives: 124 us -> 132 us  [exchange(): return lax.all_to_all(value, axes, 0, 0, tiled=True)]
    ppermute x2 -> x1, waiting for transfers between devices: 2.22 us -> 0.01 us  [body(): other = lax.ppermute(own, 'core', [(k, (k + 1) % 2) for k in range(2)])]
    dot_general x3 -> x6, matrix products: 3.95 us -> 3.88 us  [the longest x2 1.97 us: body(): jnp.einsum('jqs,jsa->qa', held, swapped, preferred_element_type=F32)]
  transfers between devices with their start and end apart: 3 -> 1, of which waited for: 1 -> 0; matrix products, arithmetic and copies ran while one was open for 1% -> 3% of each run, Pallas kernels for 0% -> 0%
where the time goes in v2:
time: 145 us
  blocking collectives  132 us (91%)
  local copies, waits for them, and re-layouts  6.64 us (5%)
  matrix products  3.88 us (3%)
  starting transfers between devices  1.91 us (1%)
    all_to_all x6, blocking collectives, exchange(): return lax.all_to_all(value, axes, 0, 0, tiled=True)  132 us
  transfers between devices with their start and end apart: 1, of which 0 were waited for; matrix products, arithmetic and copies ran while one was open for 3% of the time, Pallas kernels for 0%

profile of v2, /device:TPU:8, one launch (start us, length us, event | category | flops | bytes accessed | tf_op | source)
XLA Modules:
  0.0 144.8 jit_solution(17448646099035028432)
XLA Ops:
  0.0 1.1 copy.11
  1.1 0.9 copy.12
  2.1 18.4 %all_to_all.30 = bf16[16,2,80,128]{3,2,1,0:T(8,128)(2,1)S(1)} all-to-all(bf16[16,2,80,128]{3,2,1,0:T(8,128)(2,1)S(1)} %pad_maximum_fusion.1), channel_id=1, replica_groups=mesh['chip'=8,'core'=2,'col'=32] {'chip','core'}, dimensions={0} | all-to-all | bytes 1310720 | tf_op jit(solution)/shard_map/all_to_all | solution.py:11
  20.4 37.1 %all_to_all.31 = bf16[32,80,128]{2,1,0:T(8,128)(2,1)S(1)} all-to-all(bf16[32,80,128]{2,1,0:T(8,128)(2,1)S(1)} %bitcast.61), channel_id=1, replica_groups=mesh['chip'=8,'core'=2,'col'=32] {'col'}, dimensions={0} | all-to-all | bytes 1310720 | tf_op jit(solution)/shard_map/all_to_all | solution.py:11
  57.6 0.1 slice.26
  57.6 0.1 broadcast_in_dim.17
  57.8 0.1 pad_maximum_fusion
  57.9 21.9 %all_to_all.32 = bf16[8,768,128]{2,1,0:T(8,128)(2,1)S(1)} all-to-all(bf16[8,768,128]{2,1,0:T(8,128)(2,1)S(1)} %pad_maximum_fusion), channel_id=1, replica_groups=mesh['chip'=8,'core'=2,'col'=32] {'chip'}, dimensions={0} | all-to-all | bytes 3145728 | tf_op jit(solution)/shard_map/all_to_all | solution.py:11
  79.8 1.0 slice.28
  80.9 1.9 %collective-permute-start = (bf16[8,512,128]{2,1,0:T(8,128)(2,1)}, bf16[8,512,128]{2,1,0:T(8,128)(2,1)S(1)}, u32[]{:S(2)}, u32[]{:S(2)}) collective-permute-start(bf16[8,512,128]{2,1,0:T(8,128)(2,1)} %slice.28), channel_id=1, source_target_pairs={{0,32},{32,0},{1,33},{33,1},{2,34},{34,2},{3,35},{35,3},{4,36},{36... | collective-permute-start | bytes 3145736 | tf_op jit(solution)/shard_map/ppermute | solution.py:41
  82.9 4.2 %all_to_all.33 = bf16[2,1024,128]{2,1,0:T(8,128)(2,1)S(1)} all-to-all(bf16[2,1024,128]{2,1,0:T(8,128)(2,1)S(1)} %bitcast.64), channel_id=1, replica_groups=mesh['chip'=8,'core'=2,'col'=32] {'core'}, dimensions={0} | all-to-all | bytes 1048576 | tf_op jit(solution)/shard_map/all_to_all | solution.py:11
  87.0 0.5 copy.14
  87.6 1.1 reshape.46
  88.7 0.0 copy-start
  88.7 1.5 %convolution_bitcast_fusion.2 = f32[512,256]{1,0:T(8,128)S(1)} fusion(bf16[8,128,256]{2,1,0:T(8,128)(2,1)} %reshape.46, bf16[8,768,128]{2,1,0:T(8,128)(2,1)S(1)} %all_to_all.32), kind=kOutput, calls=%fused_computation.8 | convolution fusion | flops 268435456 | bytes 2097152 | tf_op jit(solution)/shard_map/jqs,jsa->qa/dot_general | solution.py:50
  90.3 0.0 copy-done
  90.3 0.0 copy-start.1
  90.3 0.5 fusion.6
  90.8 0.0 collective-permute-done
  90.8 0.5 copy-done.1
  91.3 0.4 convolution_bitcast_fusion
  91.8 0.5 fusion.7
  92.3 26.4 %all_to_all.34 = bf16[32,32,256]{2,1,0:T(8,128)(2,1)S(1)} all-to-all(bf16[32,32,256]{2,1,0:T(8,128)(2,1)S(1)} %bitcast.62), channel_id=1, replica_groups=mesh['chip'=8,'core'=2,'col'=32] {'col'}, dimensions={0} | all-to-all | bytes 1048576 | tf_op jit(solution)/shard_map/all_to_all | solution.py:11
  118.7 0.1 reduce_sum.12
  118.8 0.1 broadcast_in_dim.18
  118.9 24.0 %all_to_all.35 = bf16[32,32,256]{2,1,0:T(8,128)(2,1)S(1)} all-to-all(bf16[32,32,256]{2,1,0:T(8,128)(2,1)S(1)} %broadcast_in_dim.18), channel_id=1, replica_groups=mesh['chip'=8,'core'=2,'col'=32] {'col'}, dimensions={0} | all-to-all | bytes 1048576 | tf_op jit(solution)/shard_map/all_to_all | solution.py:11
  142.9 0.5 fusion.10
  143.4 0.5 fusion.1
  143.8 1.0 copy.17
  (6 shorter events, 0.2 us)
Async XLA Ops:
  80.9 9.9 %collective-permute-start = (bf16[8,512,128]{2,1,0:T(8,128)(2,1)}, bf16[8,512,128]{2,1,0:T(8,128)(2,1)S(1)}, u32[]{:S(2)}, u32[]{:S(2)}) collective-permute-start(bf16[8,512,128]{2,1,0:T(8,128)(2,1)} %slice.28), channel_id=1, source_target_pairs={{0,32},{32,0},{1,33},{33,1},{2,34},{34,2},{3,35},{35,3},{4,36},{36... | collective-permute-start | bytes 3145736 | tf_op jit(solution)/shard_map/ppermute | solution.py:41
  88.7 1.5 %copy-start = (bf16[1,8,256,128]{3,2,1,0:T(8,128)(2,1)S(1)}, bf16[1,8,256,128]{3,2,1,0:T(8,128)(2,1)}, u32[]{:S(2)}) copy-start(bf16[1,8,256,128]{3,2,1,0:T(8,128)(2,1)} %param.2) | copy-start | bytes 1572868
  90.3 1.0 copy-start.1

commit v3 on v1

v3 whole, which is shorter than its diff:
```python
import jax
import jax.numpy as jnp
from jax import lax
from jax.sharding import Mesh, PartitionSpec as P

F32 = jnp.float32
BF16 = jnp.bfloat16
ROW = ("chip", "core")


def exchange(value, axes):
    return lax.all_to_all(value, axes, 0, 0, tiled=True)


def body(amplitudes, factors):
    cores = lax.axis_size("core")
    chips = lax.axis_size("chip")
    cols = lax.axis_size("col")
    rows = chips * cores
    _, nj, block_a, block_b = amplitudes.shape
    block_q = factors.shape[0]
    half = block_b // 2
    odd = lax.rem(lax.axis_index("col"), 2)
    t = amplitudes[0]

    by_j = jnp.transpose(factors, (1, 0, 2))
    first, second = by_j[:, :, :block_b], by_j[:, :, block_b:]
    got = []
    for flip in range(2):
        pairs = [
            (r * cols + c, (c // 2) * cols + 2 * r + ((c % 2) ^ flip))
            for r in range(rows)
            for c in range(cols)
        ]
        got.append(lax.ppermute(jnp.where(odd == flip, first, second), ROW + ("col",), pairs))
    low = jnp.where(odd == 0, got[0], got[1])
    high = jnp.where(odd == 0, got[1], got[0])
    own = jnp.concatenate([low, high], axis=1)

    x = jnp.transpose(t.reshape(nj, 2, 2, half, block_b), (0, 2, 1, 3, 4))
    x = exchange(x.reshape(rows, 2 * half, block_b), ROW)

    held = [own]
    for step in range(1, chips):
        held.append(lax.ppermute(own, "chip", [(i, i ^ step) for i in range(chips)]))
    mine = jnp.stack(held)
    theirs = lax.ppermute(mine, "core", [(0, 1), (1, 0)])

    x = exchange(x.reshape(cols, half, block_b), "col")
    x = exchange(x.reshape(rows, 2 * half, block_b), ROW)
    x = x.reshape(nj, 2, 2, half, block_b)
    swapped = jnp.transpose(x, (0, 1, 3, 2, 4)).reshape(nj, block_b, block_a)

    pieces = []
    for part in (mine, theirs):
        direct = jnp.einsum("jab,sjqb->sqa", t, part, preferred_element_type=F32)
        mirror = jnp.einsum("sjqv,jva->sqa", part, swapped, preferred_element_type=F32)
        pieces.append((2.0 * direct - mirror).astype(BF16))
    parts = jnp.concatenate(pieces, axis=0).reshape(cols, block_q, block_a)

    parts = exchange(parts, "col")
    shard = jnp.sum(parts.astype(F32), axis=0).astype(BF16)
    copies = jnp.broadcast_to(shard[None], (cols, block_q, block_a))
    fitted = exchange(copies, "col").reshape(2, chips, 2 * block_q, block_a)

    result = jnp.einsum("sqa,sjqb->jab", fitted[0], mine, preferred_element_type=F32)
    result = result + jnp.einsum("sqa,sjqb->jab", fitted[1], theirs, preferred_element_type=F32)
    return result.astype(BF16)[None]


def solution(mesh):
    rows, cols = mesh.devices.shape
    fine = Mesh(mesh.devices.reshape(rows // 2, 2, cols), ("chip", "core", "col"))
    placed = (P(None, None, ROW, "col"), P("col", None, ROW))
    return jax.shard_map(
        body, mesh=fine, in_specs=placed, out_specs=P(None, None, ROW, "col"), check_vma=False
    )
```

time: 159 us -> 154 us (0.969)
  blocking collectives: 124 us -> 48.5 us
  starting transfers between devices: 10.4 us -> 68.6 us
  waiting for transfers between devices: 2.26 us -> 27.9 us
  between operations: 13.5 us -> 0.36 us
    all_to_all x5 -> x2, blocking collectives: 124 us -> 48.5 us  [exchange(): return lax.all_to_all(value, axes, 0, 0, tiled=True)]
    ppermute x2 -> x10, starting transfers between devices: 10.4 us -> 43 us  [the longest x7 30.3 us: body(): lax.ppermute(own, 'chip', [(i, i ^ step) for i in range(chips)])]
    all_to_all x0 -> x3, starting transfers between devices: none -> 25.6 us  [exchange(): return lax.all_to_all(value, axes, 0, 0, tiled=True)]
    all_to_all x0 -> x3, waiting for transfers between devices: none -> 14.6 us  [exchange(): return lax.all_to_all(value, axes, 0, 0, tiled=True)]
    ppermute x2 -> x10, waiting for transfers between devices: 2.22 us -> 13.3 us  [the longest x2 8.97 us: body(): lax.ppermute(jnp.where(odd == flip, first, second), ROW + ('col',), pairs)]
    dot_general x3 -> x6, matrix products: 3.95 us -> 2.78 us  [the longest x2 0.94 us: body(): direct = jnp.einsum('jab,sjqb->sqa', t, part, preferred_element_type=F32)]
  transfers between devices with their start and end apart: 3 -> 13, of which waited for: 1 -> 4; matrix products, arithmetic and copies ran while one was open for 1% -> 1% of each run, Pallas kernels for 0% -> 0%
where the time goes in v3:
time: 154 us; the launch traced here: 153 us
  starting transfers between devices  68.6 us (45%)
  blocking collectives  48.5 us (31%)
  waiting for transfers between devices  27.9 us (18%)
  local copies, waits for them, and re-layouts  4.6 us (3%)
  matrix products  2.78 us (2%)
    all_to_all x2, blocking collectives, exchange(): return lax.all_to_all(value, axes, 0, 0, tiled=True)  48.5 us
    ppermute x7, starting transfers between devices, body(): lax.ppermute(own, 'chip', [(i, i ^ step) for i in range(chips)])  30.3 us
    all_to_all x3, starting transfers between devices, exchange(): return lax.all_to_all(value, axes, 0, 0, tiled=True)  25.6 us
    all_to_all x3, waiting for transfers between devices, exchange(): return lax.all_to_all(value, axes, 0, 0, tiled=True)  14.6 us
    ppermute x2, starting transfers between devices, body(): lax.ppermute(jnp.where(odd == flip, first, second), ROW + ('col',), pairs)  10.4 us
    ppermute x2, waiting for transfers between devices, body(): lax.ppermute(jnp.where(odd == flip, first, second), ROW + ('col',), pairs)  8.97 us
    ppermute x7, waiting for transfers between devices, body(): lax.ppermute(own, 'chip', [(i, i ^ step) for i in range(chips)])  4.36 us
  transfers between devices with their start and end apart: 13, of which 4 were waited for; matrix products, arithmetic and copies ran while one was open for 1% of the time, Pallas kernels for 0%

profile of v3, /device:TPU:8, one launch (start us, length us, event | category | flops | bytes accessed | tf_op | source)
XLA Modules:
  0.0 152.9 jit_solution(3787664645551125476)
XLA Ops:
  0.0 1.9 %copy.13 = bf16[8,2,2,64,128]{4,3,2,1,0:T(8,128)(2,1)} copy(bf16[8,2,2,64,128]{4,3,1,2,0:T(8,128)(2,1)} %bitcast.93) | data formatting | bytes 1048576 | tf_op jit(solution)/shard_map/transpose | solution.py:40
  1.9 6.4 %all-to-all-start = ((bf16[16,128,128]{2,1,0:T(8,128)(2,1)}), bf16[16,128,128]{2,1,0:T(8,128)(2,1)}, u32[]{:S(2)}, u32[]{:S(2)}) async-start(bf16[16,128,128]{2,1,0:T(8,128)(2,1)} %bitcast.15), calls=%async_computation | async-start | bytes 1048576 | tf_op jit(solution)/shard_map/all_to_all | solution.py:12
  8.4 6.9 %collective-permute-start = (bf16[8,32,128]{2,1,0:T(8,128)(2,1)S(1)}, bf16[8,32,128]{2,1,0:T(8,128)(2,1)S(1)}, u32[]{:S(2)}, u32[]{:S(2)}) collective-permute-start(bf16[8,32,128]{2,1,0:T(8,128)(2,1)S(1)} %get-tuple-element.9), channel_id=1, source_target_pairs={{0,0},{1,1},{2,32},{3,33},{4,64},{5,65},{6,96},{7,97},{8,128},{9,1... | collective-permute-start | bytes 196616 | tf_op jit(solution)/shard_map/ppermute | solution.py:35
  15.3 3.5 %collective-permute-start.1 = (bf16[8,32,128]{2,1,0:T(8,128)(2,1)S(1)}, bf16[8,32,128]{2,1,0:T(8,128)(2,1)S(1)}, u32[]{:S(2)}, u32[]{:S(2)}) collective-permute-start(bf16[8,32,128]{2,1,0:T(8,128)(2,1)S(1)} %get-tuple-element.10), channel_id=1, source_target_pairs={{0,1},{1,0},{2,33},{3,32},{4,65},{5,64},{6,97},{7,96},{8,129},{9,1... | collective-permute-start | bytes 196616 | tf_op jit(solution)/shard_map/ppermute | solution.py:35
  18.7 9.0 %collective-permute-done.1 = bf16[8,32,128]{2,1,0:T(8,128)(2,1)S(1)} collective-permute-done((bf16[8,32,128]{2,1,0:T(8,128)(2,1)S(1)}, bf16[8,32,128]{2,1,0:T(8,128)(2,1)S(1)}, u32[]{:S(2)}, u32[]{:S(2)}) %collective-permute-start.1) | collective-permute-done | bytes 65568 | tf_op jit(solution)/shard_map/ppermute | solution.py:35
  27.8 1.9 %collective-permute-start.2 = (bf16[8,64,128]{2,1,0:T(8,128)(2,1)S(1)}, bf16[8,64,128]{2,1,0:T(8,128)(2,1)S(1)}, u32[]{:S(2)}, u32[]{:S(2)}) collective-permute-start(bf16[8,64,128]{2,1,0:T(8,128)(2,1)S(1)} %pad_maximum_fusion.1), channel_id=1, source_target_pairs={{0,64},{64,0},{128,192},{192,128},{256,320},{320,256},{384,448},{4... | collective-permute-start | bytes 393224 | tf_op jit(solution)/shard_map/ppermute | solution.py:45
  29.7 11.8 %collective-permute-start.7 = (bf16[8,64,128]{2,1,0:T(8,128)(2,1)S(1)}, bf16[8,64,128]{2,1,0:T(8,128)(2,1)S(1)}, u32[]{:S(2)}, u32[]{:S(2)}) collective-permute-start(bf16[8,64,128]{2,1,0:T(8,128)(2,1)S(1)} %pad_maximum_fusion.1), channel_id=1, source_target_pairs={{0,384},{64,448},{128,256},{192,320},{256,128},{320,192},{384,0},{... | collective-permute-start | bytes 393224 | tf_op jit(solution)/shard_map/ppermute | solution.py:45
  41.5 1.9 %collective-permute-start.6 = (bf16[8,64,128]{2,1,0:T(8,128)(2,1)S(1)}, bf16[8,64,128]{2,1,0:T(8,128)(2,1)S(1)}, u32[]{:S(2)}, u32[]{:S(2)}) collective-permute-start(bf16[8,64,128]{2,1,0:T(8,128)(2,1)S(1)} %pad_maximum_fusion.1), channel_id=1, source_target_pairs={{0,320},{64,256},{128,448},{192,384},{256,64},{320,0},{384,192},{4... | collective-permute-start | bytes 393224 | tf_op jit(solution)/shard_map/ppermute | solution.py:45
  43.5 2.8 %collective-permute-start.5 = (bf16[8,64,128]{2,1,0:T(8,128)(2,1)S(1)}, bf16[8,64,128]{2,1,0:T(8,128)(2,1)S(1)}, u32[]{:S(2)}, u32[]{:S(2)}) collective-permute-start(bf16[8,64,128]{2,1,0:T(8,128)(2,1)S(1)} %pad_maximum_fusion.1), channel_id=1, source_target_pairs={{0,256},{64,320},{128,384},{192,448},{256,0},{320,64},{384,128},{4... | collective-permute-start | bytes 393224 | tf_op jit(solution)/shard_map/ppermute | solution.py:45
  46.2 2.4 %collective-permute-start.4 = (bf16[8,64,128]{2,1,0:T(8,128)(2,1)S(1)}, bf16[8,64,128]{2,1,0:T(8,128)(2,1)S(1)}, u32[]{:S(2)}, u32[]{:S(2)}) collective-permute-start(bf16[8,64,128]{2,1,0:T(8,128)(2,1)S(1)} %pad_maximum_fusion.1), channel_id=1, source_target_pairs={{0,192},{64,128},{128,64},{192,0},{256,448},{320,384},{384,320},{4... | collective-permute-start | bytes 393224 | tf_op jit(solution)/shard_map/ppermute | solution.py:45
  48.7 15.4 %all-to-all-start.1 = ((bf16[32,64,128]{2,1,0:T(8,128)(2,1)}), bf16[32,64,128]{2,1,0:T(8,128)(2,1)}, u32[]{:S(2)}, u32[]{:S(2)}) async-start(bf16[32,64,128]{2,1,0:T(8,128)(2,1)} %bitcast.16), calls=%async_computation.1 | async-start | bytes 1048576 | tf_op jit(solution)/shard_map/all_to_all | solution.py:12
  64.1 5.1 %collective-permute-start.3 = (bf16[8,64,128]{2,1,0:T(8,128)(2,1)S(1)}, bf16[8,64,128]{2,1,0:T(8,128)(2,1)S(1)}, u32[]{:S(2)}, u32[]{:S(2)}) collective-permute-start(bf16[8,64,128]{2,1,0:T(8,128)(2,1)S(1)} %pad_maximum_fusion.1), channel_id=1, source_target_pairs={{0,128},{64,192},{128,0},{192,64},{256,384},{320,448},{384,256},{4... | collective-permute-start | bytes 393224 | tf_op jit(solution)/shard_map/ppermute | solution.py:45
  69.2 4.3 %collective-permute-done.3 = bf16[8,64,128]{2,1,0:T(8,128)(2,1)S(1)} collective-permute-done((bf16[8,64,128]{2,1,0:T(8,128)(2,1)S(1)}, bf16[8,64,128]{2,1,0:T(8,128)(2,1)S(1)}, u32[]{:S(2)}, u32[]{:S(2)}) %collective-permute-start.3) | collective-permute-done | bytes 131104 | tf_op jit(solution)/shard_map/ppermute | solution.py:45
  73.5 4.4 %collective-permute-start.8 = (bf16[8,64,128]{2,1,0:T(8,128)(2,1)S(1)}, bf16[8,64,128]{2,1,0:T(8,128)(2,1)S(1)}, u32[]{:S(2)}, u32[]{:S(2)}) collective-permute-start(bf16[8,64,128]{2,1,0:T(8,128)(2,1)S(1)} %pad_maximum_fusion.1), channel_id=1, source_target_pairs={{0,448},{64,384},{128,320},{192,256},{256,192},{320,128},{384,64},... | collective-permute-start | bytes 393224 | tf_op jit(solution)/shard_map/ppermute | solution.py:45
  78.1 6.1 %all-to-all-done.1 = bf16[32,64,128]{2,1,0:T(8,128)(2,1)} async-done(((bf16[32,64,128]{2,1,0:T(8,128)(2,1)}), bf16[32,64,128]{2,1,0:T(8,128)(2,1)}, u32[]{:S(2)}, u32[]{:S(2)}) %all-to-all-start.1) | async-done | bytes 524320 | tf_op jit(solution)/shard_map/all_to_all | solution.py:12
  84.3 3.8 %all-to-all-start.2 = ((bf16[16,128,128]{2,1,0:T(8,128)(2,1)}), bf16[16,128,128]{2,1,0:T(8,128)(2,1)S(1)}, u32[]{:S(2)}, u32[]{:S(2)}) async-start(bf16[16,128,128]{2,1,0:T(8,128)(2,1)} %bitcast.17), calls=%async_computation.2 | async-start | bytes 1048576 | tf_op jit(solution)/shard_map/all_to_all | solution.py:12
  88.1 2.3 %collective-permute-start.9 = (bf16[8,8,64,128]{3,2,1,0:T(8,128)(2,1)S(1)}, bf16[8,8,64,128]{3,2,1,0:T(8,128)(2,1)S(1)}, u32[]{:S(2)}, u32[]{:S(2)}) collective-permute-start(bf16[8,8,64,128]{3,2,1,0:T(8,128)(2,1)S(1)} %bitcast_dynamic-update-slice_fusion), channel_id=1, source_target_pairs={{0,32},{32,0},{1,33},{33,1},{2,34},{34,2},{3,35},{35,3},{4,36},{36... | collective-permute-start | bytes 3145736 | tf_op jit(solution)/shard_map/ppermute | solution.py:47
  90.4 8.5 %all-to-all-done.2 = bf16[16,128,128]{2,1,0:T(8,128)(2,1)S(1)} async-done(((bf16[16,128,128]{2,1,0:T(8,128)(2,1)}), bf16[16,128,128]{2,1,0:T(8,128)(2,1)S(1)}, u32[]{:S(2)}, u32[]{:S(2)}) %all-to-all-start.2) | async-done | bytes 524320 | tf_op jit(solution)/shard_map/all_to_all | solution.py:12
  98.9 0.5 copy.14
  99.4 0.3 reshape.32
  99.8 0.4 convolution_bitcast_fusion.4
  100.2 0.6 copy-done
  100.8 0.5 fusion.7
  101.3 0.4 convolution_bitcast_fusion.2
  101.8 0.5 fusion.8
  102.3 24.8 %all_to_all.25 = bf16[32,32,256]{2,1,0:T(8,128)(2,1)S(1)} all-to-all(bf16[32,32,256]{2,1,0:T(8,128)(2,1)S(1)} %bitcast.95), channel_id=1, replica_groups=mesh['chip'=8,'core'=2,'col'=32] {'col'}, dimensions={0} | all-to-all | bytes 1048576 | tf_op jit(solution)/shard_map/all_to_all | solution.py:12
  127.1 0.1 reduce_sum.12
  127.2 0.1 broadcast_in_dim.4
  127.3 23.7 %all_to_all.26 = bf16[32,32,256]{2,1,0:T(8,128)(2,1)S(1)} all-to-all(bf16[32,32,256]{2,1,0:T(8,128)(2,1)S(1)} %broadcast_in_dim.4), channel_id=1, replica_groups=mesh['chip'=8,'core'=2,'col'=32] {'col'}, dimensions={0} | all-to-all | bytes 1048576 | tf_op jit(solution)/shard_map/all_to_all | solution.py:12
  151.0 0.5 convolution_bitcast_fusion
  151.4 0.5 fusion.2
  151.9 1.0 copy.15
  (26 shorter events, 0.3 us)
Async XLA Ops:
  1.9 6.4 %copy-start.1 = (bf16[32,8,256]{2,1,0:T(8,128)(2,1)S(1)}, bf16[32,8,256]{2,1,0:T(8,128)(2,1)}, u32[]{:S(2)}) copy-start(bf16[32,8,256]{2,1,0:T(8,128)(2,1)} %param.3) | copy-start | bytes 393220
  1.9 46.8 %all-to-all-start = ((bf16[16,128,128]{2,1,0:T(8,128)(2,1)}), bf16[16,128,128]{2,1,0:T(8,128)(2,1)}, u32[]{:S(2)}, u32[]{:S(2)}) async-start(bf16[16,128,128]{2,1,0:T(8,128)(2,1)} %bitcast.15), calls=%async_computation | async-start | bytes 1048576 | tf_op jit(solution)/shard_map/all_to_all | solution.py:12
  8.4 10.4 %collective-permute-start = (bf16[8,32,128]{2,1,0:T(8,128)(2,1)S(1)}, bf16[8,32,128]{2,1,0:T(8,128)(2,1)S(1)}, u32[]{:S(2)}, u32[]{:S(2)}) collective-permute-start(bf16[8,32,128]{2,1,0:T(8,128)(2,1)S(1)} %get-tuple-element.9), channel_id=1, source_target_pairs={{0,0},{1,1},{2,32},{3,33},{4,64},{5,65},{6,96},{7,97},{8,128},{9,1... | collective-permute-start | bytes 196616 | tf_op jit(solution)/shard_map/ppermute | solution.py:35
  15.3 12.4 %collective-permute-start.1 = (bf16[8,32,128]{2,1,0:T(8,128)(2,1)S(1)}, bf16[8,32,128]{2,1,0:T(8,128)(2,1)S(1)}, u32[]{:S(2)}, u32[]{:S(2)}) collective-permute-start(bf16[8,32,128]{2,1,0:T(8,128)(2,1)S(1)} %get-tuple-element.10), channel_id=1, source_target_pairs={{0,1},{1,0},{2,33},{3,32},{4,65},{5,64},{6,97},{7,96},{8,129},{9,1... | collective-permute-start | bytes 196616 | tf_op jit(solution)/shard_map/ppermute | solution.py:35
  27.8 36.3 %collective-permute-start.2 = (bf16[8,64,128]{2,1,0:T(8,128)(2,1)S(1)}, bf16[8,64,128]{2,1,0:T(8,128)(2,1)S(1)}, u32[]{:S(2)}, u32[]{:S(2)}) collective-permute-start(bf16[8,64,128]{2,1,0:T(8,128)(2,1)S(1)} %pad_maximum_fusion.1), channel_id=1, source_target_pairs={{0,64},{64,0},{128,192},{192,128},{256,320},{320,256},{384,448},{4... | collective-permute-start | bytes 393224 | tf_op jit(solution)/shard_map/ppermute | solution.py:45
  29.7 58.4 %collective-permute-start.7 = (bf16[8,64,128]{2,1,0:T(8,128)(2,1)S(1)}, bf16[8,64,128]{2,1,0:T(8,128)(2,1)S(1)}, u32[]{:S(2)}, u32[]{:S(2)}) collective-permute-start(bf16[8,64,128]{2,1,0:T(8,128)(2,1)S(1)} %pad_maximum_fusion.1), channel_id=1, source_target_pairs={{0,384},{64,448},{128,256},{192,320},{256,128},{320,192},{384,0},{... | collective-permute-start | bytes 393224 | tf_op jit(solution)/shard_map/ppermute | solution.py:45
  41.5 36.5 %collective-permute-start.6 = (bf16[8,64,128]{2,1,0:T(8,128)(2,1)S(1)}, bf16[8,64,128]{2,1,0:T(8,128)(2,1)S(1)}, u32[]{:S(2)}, u32[]{:S(2)}) collective-permute-start(bf16[8,64,128]{2,1,0:T(8,128)(2,1)S(1)} %pad_maximum_fusion.1), channel_id=1, source_target_pairs={{0,320},{64,256},{128,448},{192,384},{256,64},{320,0},{384,192},{4... | collective-permute-start | bytes 393224 | tf_op jit(solution)/shard_map/ppermute | solution.py:45
  43.5 34.6 %collective-permute-start.5 = (bf16[8,64,128]{2,1,0:T(8,128)(2,1)S(1)}, bf16[8,64,128]{2,1,0:T(8,128)(2,1)S(1)}, u32[]{:S(2)}, u32[]{:S(2)}) collective-permute-start(bf16[8,64,128]{2,1,0:T(8,128)(2,1)S(1)} %pad_maximum_fusion.1), channel_id=1, source_target_pairs={{0,256},{64,320},{128,384},{192,448},{256,0},{320,64},{384,128},{4... | collective-permute-start | bytes 393224 | tf_op jit(solution)/shard_map/ppermute | solution.py:45
  46.2 31.8 %collective-permute-start.4 = (bf16[8,64,128]{2,1,0:T(8,128)(2,1)S(1)}, bf16[8,64,128]{2,1,0:T(8,128)(2,1)S(1)}, u32[]{:S(2)}, u32[]{:S(2)}) collective-permute-start(bf16[8,64,128]{2,1,0:T(8,128)(2,1)S(1)} %pad_maximum_fusion.1), channel_id=1, source_target_pairs={{0,192},{64,128},{128,64},{192,0},{256,448},{320,384},{384,320},{4... | collective-permute-start | bytes 393224 | tf_op jit(solution)/shard_map/ppermute | solution.py:45
  48.7 35.6 %all-to-all-start.1 = ((bf16[32,64,128]{2,1,0:T(8,128)(2,1)}), bf16[32,64,128]{2,1,0:T(8,128)(2,1)}, u32[]{:S(2)}, u32[]{:S(2)}) async-start(bf16[32,64,128]{2,1,0:T(8,128)(2,1)} %bitcast.16), calls=%async_computation.1 | async-start | bytes 1048576 | tf_op jit(solution)/shard_map/all_to_all | solution.py:12
  64.1 9.4 %collective-permute-start.3 = (bf16[8,64,128]{2,1,0:T(8,128)(2,1)S(1)}, bf16[8,64,128]{2,1,0:T(8,128)(2,1)S(1)}, u32[]{:S(2)}, u32[]{:S(2)}) collective-permute-start(bf16[8,64,128]{2,1,0:T(8,128)(2,1)S(1)} %pad_maximum_fusion.1), channel_id=1, source_target_pairs={{0,128},{64,192},{128,0},{192,64},{256,384},{320,448},{384,256},{4... | collective-permute-start | bytes 393224 | tf_op jit(solution)/shard_map/ppermute | solution.py:45
  73.5 14.5 %collective-permute-start.8 = (bf16[8,64,128]{2,1,0:T(8,128)(2,1)S(1)}, bf16[8,64,128]{2,1,0:T(8,128)(2,1)S(1)}, u32[]{:S(2)}, u32[]{:S(2)}) collective-permute-start(bf16[8,64,128]{2,1,0:T(8,128)(2,1)S(1)} %pad_maximum_fusion.1), channel_id=1, source_target_pairs={{0,448},{64,384},{128,320},{192,256},{256,192},{320,128},{384,64},... | collective-permute-start | bytes 393224 | tf_op jit(solution)/shard_map/ppermute | solution.py:45
  84.3 14.6 %all-to-all-start.2 = ((bf16[16,128,128]{2,1,0:T(8,128)(2,1)}), bf16[16,128,128]{2,1,0:T(8,128)(2,1)S(1)}, u32[]{:S(2)}, u32[]{:S(2)}) async-start(bf16[16,128,128]{2,1,0:T(8,128)(2,1)} %bitcast.17), calls=%async_computation.2 | async-start | bytes 1048576 | tf_op jit(solution)/shard_map/all_to_all | solution.py:12
  88.1 13.2 %collective-permute-start.9 = (bf16[8,8,64,128]{3,2,1,0:T(8,128)(2,1)S(1)}, bf16[8,8,64,128]{3,2,1,0:T(8,128)(2,1)S(1)}, u32[]{:S(2)}, u32[]{:S(2)}) collective-permute-start(bf16[8,8,64,128]{3,2,1,0:T(8,128)(2,1)S(1)} %bitcast_dynamic-update-slice_fusion), channel_id=1, source_target_pairs={{0,32},{32,0},{1,33},{33,1},{2,34},{34,2},{3,35},{35,3},{4,36},{36... | collective-permute-start | bytes 3145736 | tf_op jit(solution)/shard_map/ppermute | solution.py:47
  99.8 1.0 copy-start

commit v4 on v2

v4 whole, which is shorter than its diff:
```python
import jax
import jax.numpy as jnp
from jax import lax
from jax.sharding import Mesh, PartitionSpec as P

F32 = jnp.float32
BF16 = jnp.bfloat16
ROW = ("chip", "core")
SWAP = [(0, 1), (1, 0)]


def exchange(value, axes):
    return lax.all_to_all(value, axes, 0, 0, tiled=True)


def in_core_order(core, mine, theirs):
    first = jnp.where(core == 0, mine, theirs)
    second = jnp.where(core == 0, theirs, mine)
    return first, second


def body(amplitudes, factors):
    core = lax.axis_index("core")
    chips = lax.axis_size("chip")
    cols = lax.axis_size("col")
    _, nj, block_a, block_b = amplitudes.shape
    block_q = factors.shape[0]
    aux = block_q * cols
    half = block_b // 2
    few = block_q // 2
    per_core = nj // 2
    t = amplitudes[0].reshape(2, per_core, block_a, block_b)

    x = jnp.transpose(t.reshape(2, per_core, 2, 2, half, block_b), (1, 3, 0, 2, 4, 5))
    x = x.reshape(chips * 2, 2, half, block_b)
    y = jnp.transpose(factors.reshape(2, few, 2, per_core, 2, block_b), (3, 0, 2, 4, 1, 5))
    y = y.reshape(chips * 2, 2, few, block_b)
    both = exchange(jnp.concatenate([x, y], axis=2), ROW)
    both = exchange(both.reshape(cols, half + few, block_b), "col")
    x, y = both[:, :half], both[:, half:]

    sent = jnp.where(core == 0, t[1], t[0])
    kept = jnp.where(core == 0, t[0], t[1])
    straight = in_core_order(core, kept, lax.ppermute(sent, "core", SWAP))

    x = x.reshape(chips, 4 * half, block_b)
    y = jnp.broadcast_to(y.reshape(1, cols * few, block_b), (chips, cols * few, block_b))
    both = exchange(jnp.concatenate([x, y], axis=1), "chip")
    mine = both[:, 4 * half :].reshape(per_core, aux, block_b)
    x = both[:, : 4 * half].reshape(per_core, 2, 2, 2, half, block_b)
    swapped = jnp.transpose(x, (2, 0, 1, 4, 3, 5)).reshape(2, per_core, block_b, block_a)

    pieces = []
    for h in range(2):
        direct = jnp.einsum("jab,jqb->qa", straight[h], mine, preferred_element_type=F32)
        mirror = jnp.einsum("jqv,jva->qa", mine, swapped[h], preferred_element_type=F32)
        pieces.append((2.0 * direct - mirror).astype(BF16))
    pieces = exchange(jnp.stack(pieces), "core")
    partial = (pieces[0].astype(F32) + pieces[1].astype(F32)).astype(BF16)

    theirs = lax.ppermute(mine, "core", SWAP)
    low, high = in_core_order(core, mine, theirs)

    parts = exchange(partial.reshape(cols, block_q, block_a), "col")
    shard = jnp.sum(parts.astype(F32), axis=0).astype(BF16)
    copies = jnp.broadcast_to(shard[None], (cols, block_q, block_a))
    fitted = exchange(copies, "col").reshape(aux, block_a)

    held = jnp.concatenate([low, high], axis=0)
    result = jnp.einsum("qa,jqb->jab", fitted, held, preferred_element_type=F32)
    return result.astype(BF16)[None]


def solution(mesh):
    rows, cols = mesh.devices.shape
    fine = Mesh(mesh.devices.reshape(rows // 2, 2, cols), ("chip", "core", "col"))
    placed = (P(None, None, ROW, "col"), P("col", None, ROW))
    return jax.shard_map(
        body, mesh=fine, in_specs=placed, out_specs=P(None, None, ROW, "col"), check_vma=False
    )
```

time: 145 us -> 148 us (1.021)
  blocking collectives: 132 us -> 60 us
  waiting for transfers between devices: 0.01 us -> 51 us
  starting transfers between devices: 1.91 us -> 19.7 us
  other arithmetic: 0.27 us -> 4.63 us
    all_to_all x6 -> x3, blocking collectives: 132 us -> 60 us  [exchange(): return lax.all_to_all(value, axes, 0, 0, tiled=True)]
    all_to_all x0 -> x3, waiting for transfers between devices: none -> 51 us  [exchange(): return lax.all_to_all(value, axes, 0, 0, tiled=True)]
    all_to_all x0 -> x3, starting transfers between devices: none -> 15.9 us  [exchange(): return lax.all_to_all(value, axes, 0, 0, tiled=True)]
    select_n x0 -> x2, other arithmetic: none -> 2.21 us  [the longest x1 1.48 us: in_core_order(): first = jnp.where(core == 0, mine, theirs)]
    ppermute x1 -> x2, starting transfers between devices: 1.91 us -> 3.83 us  [the longest x1 1.92 us: body(): theirs = lax.ppermute(mine, 'core', SWAP)]
    dot_general x6 -> x5, matrix products: 3.88 us -> 4.11 us  [the longest x1 2.3 us: body(): result = jnp.einsum('qa,jqb->jab', fitted, held, preferred_element_type=F32)]
  transfers between devices with their start and end apart: 1 -> 5, of which waited for: 0 -> 3; matrix products, arithmetic and copies ran while one was open for 3% -> 5% of each run, Pallas kernels for 0% -> 0%
where the time goes in v4:
time: 148 us
  blocking collectives  60 us (41%)
  waiting for transfers between devices  51 us (34%)
  starting transfers between devices  19.7 us (13%)
  local copies, waits for them, and re-layouts  7.86 us (5%)
  other arithmetic  4.63 us (3%)
  matrix products  4.11 us (3%)
    all_to_all x3, blocking collectives, exchange(): return lax.all_to_all(value, axes, 0, 0, tiled=True)  60 us
    all_to_all x3, waiting for transfers between devices, exchange(): return lax.all_to_all(value, axes, 0, 0, tiled=True)  51 us
    all_to_all x3, starting transfers between devices, exchange(): return lax.all_to_all(value, axes, 0, 0, tiled=True)  15.9 us
  transfers between devices with their start and end apart: 5, of which 3 were waited for; matrix products, arithmetic and copies ran while one was open for 5% of the time, Pallas kernels for 0%

profile of v4, /device:TPU:8, one launch (start us, length us, event | category | flops | bytes accessed | tf_op | source)
XLA Modules:
  0.0 147.6 jit_solution(13403066591071414065)
XLA Ops:
  0.0 0.9 reshape.48
  1.0 1.1 copy.9
  2.1 18.4 %all_to_all.30 = bf16[16,2,80,128]{3,2,1,0:T(8,128)(2,1)S(1)} all-to-all(bf16[16,2,80,128]{3,2,1,0:T(8,128)(2,1)S(1)} %pad_maximum_fusion.2), channel_id=1, replica_groups=mesh['chip'=8,'core'=2,'col'=32] {'chip','core'}, dimensions={0} | all-to-all | bytes 1310720 | tf_op jit(solution)/shard_map/all_to_all | solution.py:13
  20.5 37.1 %all_to_all.31 = bf16[32,80,128]{2,1,0:T(8,128)(2,1)S(1)} all-to-all(bf16[32,80,128]{2,1,0:T(8,128)(2,1)S(1)} %bitcast.74), channel_id=1, replica_groups=mesh['chip'=8,'core'=2,'col'=32] {'col'}, dimensions={0} | all-to-all | bytes 1310720 | tf_op jit(solution)/shard_map/all_to_all | solution.py:13
  57.7 0.1 broadcast_in_dim.17
  57.8 1.3 pad_maximum_fusion
  59.1 3.7 %all-to-all-start.2 = ((bf16[8,768,128]{2,1,0:T(8,128)(2,1)}), bf16[8,768,128]{2,1,0:T(8,128)(2,1)S(1)}, u32[]{:S(2)}, u32[]{:S(2)}) async-start(bf16[8,768,128]{2,1,0:T(8,128)(2,1)} %pad_maximum_fusion), calls=%async_computation.2 | async-start | bytes 3145728 | tf_op jit(solution)/shard_map/all_to_all | solution.py:13
  62.8 0.7 select_bitcast_fusion
  63.6 1.9 %collective-permute-start.1 = (bf16[4,256,128]{2,1,0:T(8,128)(2,1)}, bf16[4,256,128]{2,1,0:T(8,128)(2,1)S(1)}, u32[]{:S(2)}, u32[]{:S(2)}) collective-permute-start(bf16[4,256,128]{2,1,0:T(8,128)(2,1)} %select_bitcast_fusion), channel_id=1, source_target_pairs={{0,32},{32,0},{1,33},{33,1},{2,34},{34,2},{3,35},{35,3},{4,36},{36... | collective-permute-start | bytes 786440 | tf_op jit(solution)/shard_map/ppermute | solution.py:44
  65.5 15.4 %all-to-all-done.2 = bf16[8,768,128]{2,1,0:T(8,128)(2,1)S(1)} async-done(((bf16[8,768,128]{2,1,0:T(8,128)(2,1)}), bf16[8,768,128]{2,1,0:T(8,128)(2,1)S(1)}, u32[]{:S(2)}, u32[]{:S(2)}) %all-to-all-start.2) | async-done | bytes 1572896 | tf_op jit(solution)/shard_map/all_to_all | solution.py:13
  80.9 0.5 copy.16
  81.5 1.2 fusion.21
  82.6 0.9 squeeze.5
  83.6 0.9 copy-done.1
  84.5 0.4 convolution_bitcast_fusion
  84.9 0.2 squeeze.4
  85.1 0.4 convolution_bitcast_fusion.2
  85.5 0.5 fusion.17
  86.0 0.5 fusion.16
  86.5 0.1 pad_maximum_fusion.1
  86.6 4.6 %all_to_all.32 = bf16[2,1024,256]{2,1,0:T(8,128)(2,1)S(1)} all-to-all(bf16[2,1024,256]{2,1,0:T(8,128)(2,1)S(1)} %pad_maximum_fusion.1), channel_id=1, replica_groups=mesh['chip'=8,'core'=2,'col'=32] {'core'}, dimensions={0} | all-to-all | bytes 2097152 | tf_op jit(solution)/shard_map/all_to_all | solution.py:13
  91.2 0.9 add_convert_fusion
  92.1 7.1 %all-to-all-start.4 = ((bf16[32,32,256]{2,1,0:T(8,128)(2,1)}), bf16[32,32,256]{2,1,0:T(8,128)(2,1)S(1)}, u32[]{:S(2)}, u32[]{:S(2)}) async-start(bf16[32,32,256]{2,1,0:T(8,128)(2,1)} %bitcast.19), calls=%async_computation.4 | async-start | bytes 1048576 | tf_op jit(solution)/shard_map/all_to_all | solution.py:13
  99.2 1.9 %collective-permute-start = (bf16[4,1024,128]{2,1,0:T(8,128)(2,1)S(1)}, bf16[4,1024,128]{2,1,0:T(8,128)(2,1)S(1)}, u32[]{:S(2)}, u32[]{:S(2)}) collective-permute-start(bf16[4,1024,128]{2,1,0:T(8,128)(2,1)S(1)} %bitcast.71), channel_id=1, source_target_pairs={{0,32},{32,0},{1,33},{33,1},{2,34},{34,2},{3,35},{35,3},{4,36},{36... | collective-permute-start | bytes 3145736 | tf_op jit(solution)/shard_map/ppermute | solution.py:61
  101.2 17.8 %all-to-all-done.4 = bf16[32,32,256]{2,1,0:T(8,128)(2,1)S(1)} async-done(((bf16[32,32,256]{2,1,0:T(8,128)(2,1)}), bf16[32,32,256]{2,1,0:T(8,128)(2,1)S(1)}, u32[]{:S(2)}, u32[]{:S(2)}) %all-to-all-start.4) | async-done | bytes 524320 | tf_op jit(solution)/shard_map/all_to_all | solution.py:13
  118.9 0.1 reduce_sum.12
  119.0 0.9 broadcast_in_dim.18
  119.9 5.1 %all-to-all-start.5 = ((bf16[32,32,256]{2,1,0:T(8,128)(2,1)}), bf16[32,32,256]{2,1,0:T(8,128)(2,1)S(1)}, u32[]{:S(2)}, u32[]{:S(2)}) async-start(bf16[32,32,256]{2,1,0:T(8,128)(2,1)} %broadcast_in_dim.18), calls=%async_computation.5 | async-start | bytes 1048576 | tf_op jit(solution)/shard_map/all_to_all | solution.py:13
  125.0 1.5 broadcast_select_fusion.1
  126.4 17.9 %all-to-all-done.5 = bf16[32,32,256]{2,1,0:T(8,128)(2,1)S(1)} async-done(((bf16[32,32,256]{2,1,0:T(8,128)(2,1)}), bf16[32,32,256]{2,1,0:T(8,128)(2,1)S(1)}, u32[]{:S(2)}, u32[]{:S(2)}) %all-to-all-start.5) | async-done | bytes 524320 | tf_op jit(solution)/shard_map/all_to_all | solution.py:13
  144.3 2.3 %fusion.13 = bf16[1,8,256,128]{2,3,1,0:T(8,128)(2,1)S(1)} fusion(bf16[1024,256,1]{1,0,2:T(8,128)(2,1)S(1)} %bitcast.81, bf16[4,1024,128]{2,1,0:T(8,128)(2,1)} %get-tuple-element.6, bf16[4,1024,128]{2,1,0:T(8,128)(2,1)} %get-tuple-element.5), kind=kOutput, calls=%fused_computation.16 | convolution fusion | flops 538181632 | bytes 3145728 | tf_op jit(solution)/shard_map/qa,jqb->jab/dot_general | solution.py:70
  146.6 1.0 copy.13
  (13 shorter events, 0.3 us)
Async XLA Ops:
  59.1 3.7 %copy-start = (bf16[1,8,256,128]{3,2,1,0:T(8,128)(2,1)S(1)}, bf16[1,8,256,128]{3,2,1,0:T(8,128)(2,1)}, u32[]{:S(2)}) copy-start(bf16[1,8,256,128]{3,2,1,0:T(8,128)(2,1)} %param.2) | copy-start | bytes 1572868
  59.1 21.8 %all-to-all-start.2 = ((bf16[8,768,128]{2,1,0:T(8,128)(2,1)}), bf16[8,768,128]{2,1,0:T(8,128)(2,1)S(1)}, u32[]{:S(2)}, u32[]{:S(2)}) async-start(bf16[8,768,128]{2,1,0:T(8,128)(2,1)} %pad_maximum_fusion), calls=%async_computation.2 | async-start | bytes 3145728 | tf_op jit(solution)/shard_map/all_to_all | solution.py:13
  63.6 22.0 %collective-permute-start.1 = (bf16[4,256,128]{2,1,0:T(8,128)(2,1)}, bf16[4,256,128]{2,1,0:T(8,128)(2,1)S(1)}, u32[]{:S(2)}, u32[]{:S(2)}) collective-permute-start(bf16[4,256,128]{2,1,0:T(8,128)(2,1)} %select_bitcast_fusion), channel_id=1, source_target_pairs={{0,32},{32,0},{1,33},{33,1},{2,34},{34,2},{3,35},{35,3},{4,36},{36... | collective-permute-start | bytes 786440 | tf_op jit(solution)/shard_map/ppermute | solution.py:44
  83.5 0.9 copy-start.1
  83.6 1.3 copy-start.2
  92.1 26.8 %all-to-all-start.4 = ((bf16[32,32,256]{2,1,0:T(8,128)(2,1)}), bf16[32,32,256]{2,1,0:T(8,128)(2,1)S(1)}, u32[]{:S(2)}, u32[]{:S(2)}) async-start(bf16[32,32,256]{2,1,0:T(8,128)(2,1)} %bitcast.19), calls=%async_computation.4 | async-start | bytes 1048576 | tf_op jit(solution)/shard_map/all_to_all | solution.py:13
  99.2 25.7 %collective-permute-start = (bf16[4,1024,128]{2,1,0:T(8,128)(2,1)S(1)}, bf16[4,1024,128]{2,1,0:T(8,128)(2,1)S(1)}, u32[]{:S(2)}, u32[]{:S(2)}) collective-permute-start(bf16[4,1024,128]{2,1,0:T(8,128)(2,1)S(1)} %bitcast.71), channel_id=1, source_target_pairs={{0,32},{32,0},{1,33},{33,1},{2,34},{34,2},{3,35},{35,3},{4,36},{36... | collective-permute-start | bytes 3145736 | tf_op jit(solution)/shard_map/ppermute | solution.py:61
  119.9 24.4 %all-to-all-start.5 = ((bf16[32,32,256]{2,1,0:T(8,128)(2,1)}), bf16[32,32,256]{2,1,0:T(8,128)(2,1)S(1)}, u32[]{:S(2)}, u32[]{:S(2)}) async-start(bf16[32,32,256]{2,1,0:T(8,128)(2,1)} %broadcast_in_dim.18), calls=%async_computation.5 | async-start | bytes 1048576 | tf_op jit(solution)/shard_map/all_to_all | solution.py:13

commit v5 on v2

v5 whole, which is shorter than its diff:
```python
import jax
import jax.numpy as jnp
from jax import lax
from jax.experimental import pallas as pl
from jax.experimental.pallas import tpu as pltpu
from jax.sharding import Mesh, PartitionSpec as P

F32 = jnp.float32
BF16 = jnp.bfloat16
ROW = ("chip", "core")
VMEM = pl.BlockSpec(memory_space=pltpu.VMEM)


def exchange(value, axes):
    return lax.all_to_all(value, axes, 0, 0, tiled=True)


def fit_kernel(both_ref, t_ref, out_ref):
    nj, block_a, block_b = t_ref.shape
    half = block_b // 2
    aux_half = both_ref.shape[2] - block_b
    straight = jnp.concatenate([t_ref[j] for j in range(nj)], axis=1)
    columns = []
    for side in range(2):
        rows = pl.ds(side * half, half)
        columns.append(
            jnp.concatenate([both_ref[s, j, rows, :] for j in range(nj) for s in range(2)], axis=0)
        )
    swapped = jnp.concatenate(columns, axis=1)
    for s in range(2):
        held = jnp.concatenate(
            [both_ref[s, j, pl.ds(block_b, aux_half), :] for j in range(nj)], axis=1
        )
        direct = lax.dot_general(
            held, straight, (((1,), (1,)), ((), ())), preferred_element_type=F32
        )
        mirror = jnp.dot(held, swapped, preferred_element_type=F32)
        out_ref[pl.ds(s * aux_half, aux_half), :] = (2.0 * direct - mirror).astype(BF16)


def body(amplitudes, factors):
    cores = lax.axis_size("core")
    chips = lax.axis_size("chip")
    cols = lax.axis_size("col")
    rows = chips * cores
    _, nj, block_a, block_b = amplitudes.shape
    block_q = factors.shape[0]
    aux = block_q * cols
    half = block_b // 2
    few = block_q // 2
    t = amplitudes[0]

    x = jnp.transpose(t.reshape(nj, 2, 2, half, block_b), (0, 2, 1, 3, 4))
    x = x.reshape(rows, 2, half, block_b)
    y = jnp.transpose(factors.reshape(2, few, nj, 2, block_b), (2, 0, 3, 1, 4))
    y = y.reshape(rows, 2, few, block_b)
    both = exchange(jnp.concatenate([x, y], axis=2), ROW)
    both = exchange(both.reshape(cols, half + few, block_b), "col")
    x, y = both[:, :half], both[:, half:]

    x = x.reshape(chips, 4 * half, block_b)
    y = jnp.broadcast_to(y.reshape(1, cols * few, block_b), (chips, cols * few, block_b))
    both = exchange(jnp.concatenate([x, y], axis=1), "chip")

    x = jnp.transpose(both[:, : 4 * half].reshape(nj, 2, block_b, block_b), (1, 0, 2, 3))
    y = jnp.broadcast_to(both[None, :, 4 * half :], (2, nj, aux // 2, block_b))
    both = exchange(jnp.concatenate([x, y], axis=2), "core")

    partial = pl.pallas_call(
        fit_kernel,
        out_shape=jax.ShapeDtypeStruct((aux, block_a), BF16),
        in_specs=[VMEM, VMEM],
        out_specs=VMEM,
        compiler_params=pltpu.CompilerParams(vmem_limit_bytes=32 << 20),
        cost_estimate=pl.CostEstimate(
            flops=4 * aux * block_a * nj * block_b, bytes_accessed=4 << 20, transcendentals=0
        ),
    )(both, t)

    parts = exchange(partial.reshape(cols, block_q, block_a), "col")
    shard = jnp.sum(parts.astype(F32), axis=0).astype(BF16)
    copies = jnp.broadcast_to(shard[None], (cols, block_q, block_a))
    fitted = exchange(copies, "col").reshape(2, aux // 2, block_a)

    held = both[:, :, block_b:]
    result = jnp.einsum("sqa,sjqb->jab", fitted, held, preferred_element_type=F32)
    return result.astype(BF16)[None]


def solution(mesh):
    rows, cols = mesh.devices.shape
    fine = Mesh(mesh.devices.reshape(rows // 2, 2, cols), ("chip", "core", "col"))
    placed = (P(None, None, ROW, "col"), P("col", None, ROW))
    return jax.shard_map(
        body, mesh=fine, in_specs=placed, out_specs=P(None, None, ROW, "col"), check_vma=False
    )
```

time: 145 us -> 141 us (0.972)
  matrix products: 3.88 us -> 0.76 us
  local copies, waits for them, and re-layouts: 6.64 us -> 3.82 us
  blocking collectives: 132 us -> 134 us
  starting transfers between devices: 1.91 us -> 0 us
    dot_general x6 -> x1, matrix products: 3.88 us -> 0.76 us  [body(): jnp.einsum('sqa,sjqb->jab', fitted, held, preferred_element_type=F32)]
    ppermute x1 -> x0, starting transfers between devices: 1.91 us -> none  [body(): other = lax.ppermute(own, 'core', [(k, (k + 1) % 2) for k in range(2)])]
    all_to_all x6, blocking collectives: 132 us -> 134 us  [exchange(): return lax.all_to_all(value, axes, 0, 0, tiled=True)]
  transfers between devices with their start and end apart: 1 -> 0, of which waited for: 0 -> 0; matrix products, arithmetic and copies ran while one was open for 3% -> 0% of each run, Pallas kernels for 0% -> 0%
where the time goes in v5:
time: 141 us; the launch traced here: 140 us
  blocking collectives  134 us (95%)
  local copies, waits for them, and re-layouts  3.82 us (3%)
    all_to_all x6, blocking collectives, exchange(): return lax.all_to_all(value, axes, 0, 0, tiled=True)  134 us

profile of v5, /device:TPU:8, one launch (start us, length us, event | category | flops | bytes accessed | tf_op | source)
XLA Modules:
  0.0 140.2 jit_solution(17174299766361086705)
XLA Ops:
  0.0 0.9 copy.9
  0.9 1.1 copy.8
  2.1 18.4 %all_to_all.30 = bf16[16,2,80,128]{3,2,1,0:T(8,128)(2,1)S(1)} all-to-all(bf16[16,2,80,128]{3,2,1,0:T(8,128)(2,1)S(1)} %pad_maximum_fusion.2), channel_id=1, replica_groups=mesh['chip'=8,'core'=2,'col'=32] {'chip','core'}, dimensions={0} | all-to-all | bytes 1310720 | tf_op jit(solution)/shard_map/all_to_all | solution.py:15
  20.4 37.1 %all_to_all.31 = bf16[32,80,128]{2,1,0:T(8,128)(2,1)S(1)} all-to-all(bf16[32,80,128]{2,1,0:T(8,128)(2,1)S(1)} %bitcast.36), channel_id=1, replica_groups=mesh['chip'=8,'core'=2,'col'=32] {'col'}, dimensions={0} | all-to-all | bytes 1310720 | tf_op jit(solution)/shard_map/all_to_all | solution.py:15
  57.6 0.1 slice.20
  57.6 0.1 broadcast_in_dim.11
  57.8 0.1 pad_maximum_fusion.1
  57.9 21.9 %all_to_all.32 = bf16[8,768,128]{2,1,0:T(8,128)(2,1)S(1)} all-to-all(bf16[8,768,128]{2,1,0:T(8,128)(2,1)S(1)} %pad_maximum_fusion.1), channel_id=1, replica_groups=mesh['chip'=8,'core'=2,'col'=32] {'chip'}, dimensions={0} | all-to-all | bytes 3145728 | tf_op jit(solution)/shard_map/all_to_all | solution.py:15
  79.9 0.1 slice.23
  80.0 0.4 broadcast_in_dim.24
  80.4 0.2 pad_maximum_fusion
  80.6 0.0 copy-start
  80.7 6.0 %all_to_all.33.both_ref = bf16[2,8,640,128]{3,2,1,0:T(8,128)(2,1)S(1)} all-to-all(bf16[2,8,640,128]{3,2,1,0:T(8,128)(2,1)S(1)} %pad_maximum_fusion), channel_id=1, replica_groups=mesh['chip'=8,'core'=2,'col'=32] {'core'}, dimensions={0} | all-to-all | bytes 5242880 | tf_op jit(solution)/shard_map/all_to_all | solution.py:15
  86.6 0.0 copy-done
  86.6 1.3 shard_map.28
  87.9 26.4 %all_to_all.34 = bf16[32,32,256]{2,1,0:T(8,128)(2,1)S(1)} all-to-all(bf16[32,32,256]{2,1,0:T(8,128)(2,1)S(1)} %bitcast.35), channel_id=1, replica_groups=mesh['chip'=8,'core'=2,'col'=32] {'col'}, dimensions={0} | all-to-all | bytes 1048576 | tf_op jit(solution)/shard_map/all_to_all | solution.py:15
  114.3 0.1 reduce_sum.12
  114.4 0.1 broadcast_in_dim.25
  114.5 24.0 %all_to_all.35 = bf16[32,32,256]{2,1,0:T(8,128)(2,1)S(1)} all-to-all(bf16[32,32,256]{2,1,0:T(8,128)(2,1)S(1)} %broadcast_in_dim.25), channel_id=1, replica_groups=mesh['chip'=8,'core'=2,'col'=32] {'col'}, dimensions={0} | all-to-all | bytes 1048576 | tf_op jit(solution)/shard_map/all_to_all | solution.py:15
  138.5 0.8 fusion.8
  139.2 1.0 copy.12
  (4 shorter events, 0.1 us)
Async XLA Ops:
  80.6 6.0 %copy-start = (bf16[1,8,256,128]{3,2,1,0:T(8,128)(2,1)S(1)}, bf16[1,8,256,128]{3,2,1,0:T(8,128)(2,1)}, u32[]{:S(2)}) copy-start(bf16[1,8,256,128]{3,2,1,0:T(8,128)(2,1)} %param.2) | copy-start | bytes 1572868

commit v6 on v5

--- a/solution.py
+++ b/solution.py
@@ -38,6 +38,52 @@
         out_ref[pl.ds(s * aux_half, aux_half), :] = (2.0 * direct - mirror).astype(BF16)
 
 
+def pack_kernel(t_ref, f_ref, out_ref):
+    nj, _, block_b = t_ref.shape
+    half = block_b // 2
+    few = f_ref.shape[0] // 2
+    for j in range(nj):
+        for bit in range(2):
+            for side in range(2):
+                rows = pl.ds(side * block_b + bit * half, half)
+                out_ref[2 * j + bit, side, pl.ds(0, half), :] = t_ref[j, rows, :]
+    for bit in range(2):
+        for side in range(2):
+            piece = f_ref[pl.ds(bit * few, few), :, pl.ds(side * block_b, block_b)]
+            by_j = jnp.swapaxes(piece.astype(F32), 0, 1).astype(BF16)
+            for j in range(nj):
+                out_ref[2 * j + bit, side, pl.ds(half, few), :] = by_j[j]
+
+
+def project_kernel(fitted_ref, both_ref, out_ref):
+    nj, _, block_b = out_ref.shape
+    aux_half = fitted_ref.shape[0] // 2
+    total = None
+    for s in range(2):
+        held = jnp.concatenate(
+            [both_ref[s, j, pl.ds(block_b, aux_half), :] for j in range(nj)], axis=1
+        )
+        term = lax.dot_general(
+            fitted_ref[pl.ds(s * aux_half, aux_half), :],
+            held,
+            (((0,), (0,)), ((), ())),
+            preferred_element_type=F32,
+        )
+        total = term if total is None else total + term
+    for j in range(nj):
+        out_ref[j] = total[:, j * block_b : (j + 1) * block_b].astype(BF16)
+
+
+def call(kernel, shape, *operands):
+    return pl.pallas_call(
+        kernel,
+        out_shape=jax.ShapeDtypeStruct(shape, BF16),
+        in_specs=[VMEM] * len(operands),
+        out_specs=VMEM,
+        compiler_params=pltpu.CompilerParams(vmem_limit_bytes=32 << 20),
+    )(*operands)
+
+
 def body(amplitudes, factors):
     cores = lax.axis_size("core")
     chips = lax.axis_size("chip")
@@ -50,11 +96,7 @@
     few = block_q // 2
     t = amplitudes[0]
 
-    x = jnp.transpose(t.reshape(nj, 2, 2, half, block_b), (0, 2, 1, 3, 4))
-    x = x.reshape(rows, 2, half, block_b)
-    y = jnp.transpose(factors.reshape(2, few, nj, 2, block_b), (2, 0, 3, 1, 4))
-    y = y.reshape(rows, 2, few, block_b)
-    both = exchange(jnp.concatenate([x, y], axis=2), ROW)
+    both = exchange(call(pack_kernel, (rows, 2, half + few, block_b), t, factors), ROW)
     both = exchange(both.reshape(cols, half + few, block_b), "col")
     x, y = both[:, :half], both[:, half:]
 
@@ -66,25 +108,14 @@
     y = jnp.broadcast_to(both[None, :, 4 * half :], (2, nj, aux // 2, block_b))
     both = exchange(jnp.concatenate([x, y], axis=2), "core")
 
-    partial = pl.pallas_call(
-        fit_kernel,
-        out_shape=jax.ShapeDtypeStruct((aux, block_a), BF16),
-        in_specs=[VMEM, VMEM],
-        out_specs=VMEM,
-        compiler_params=pltpu.CompilerParams(vmem_limit_bytes=32 << 20),
-        cost_estimate=pl.CostEstimate(
-            flops=4 * aux * block_a * nj * block_b, bytes_accessed=4 << 20, transcendentals=0
-        ),
-    )(both, t)
+    partial = call(fit_kernel, (aux, block_a), both, t)
 
     parts = exchange(partial.reshape(cols, block_q, block_a), "col")
     shard = jnp.sum(parts.astype(F32), axis=0).astype(BF16)
     copies = jnp.broadcast_to(shard[None], (cols, block_q, block_a))
-    fitted = exchange(copies, "col").reshape(2, aux // 2, block_a)
+    fitted = exchange(copies, "col").reshape(aux, block_a)
 
-    held = both[:, :, block_b:]
-    result = jnp.einsum("sqa,sjqb->jab", fitted, held, preferred_element_type=F32)
-    return result.astype(BF16)[None]
+    return call(project_kernel, (nj, block_a, block_b), fitted, both)[None]
 
 
 def solution(mesh):

time: 141 us -> 140 us (level)
  Pallas kernels: 1.26 us -> 2.87 us
    transpose x2 -> x0, local copies, waits for them, and re-layouts: 2.02 us -> none  [the longest x1 1.08 us: body(): x = jnp.transpose(t.reshape(nj, 2, 2, half, block_b), (0, 2, 1, 3, 4))]
    unnamed x2 -> x4, local copies, waits for them, and re-layouts: 0.01 us -> 1.94 us
    pallas_call x1 -> x3, Pallas kernels: 1.26 us -> 2.87 us  [call(): pl.pallas_call(kernel, out_shape=jax.ShapeDtypeStruct(shape, BF16), in_sp...]
where the time goes in v6:
time: 140 us
  blocking collectives  134 us (96%)
  Pallas kernels  2.87 us (2%)
  local copies, waits for them, and re-layouts  2.74 us (2%)
    all_to_all x6, blocking collectives, exchange(): return lax.all_to_all(value, axes, 0, 0, tiled=True)  134 us
    pallas_call x3, Pallas kernels, call(): pl.pallas_call(kernel, out_shape=jax.ShapeDtypeStruct(shape, BF16), in_sp...  2.87 us

profile of v6, /device:TPU:8, one launch (start us, length us, event | category | flops | bytes accessed | tf_op | source)
XLA Modules:
  0.0 139.8 jit_solution(12321103119126973548)
XLA Ops:
  0.0 0.0 copy-start
  0.0 1.0 copy-done
  1.0 0.0 copy-start.1
  1.0 0.9 copy-done.1
  1.9 0.1 shard_map.28
  2.0 18.4 %all_to_all.30 = bf16[16,2,80,128]{3,2,1,0:T(8,128)(2,1)S(1)} all-to-all(bf16[16,2,80,128]{3,2,1,0:T(8,128)(2,1)S(1)} %shard_map.28), channel_id=1, replica_groups=mesh['chip'=8,'core'=2,'col'=32] {'chip','core'}, dimensions={0} | all-to-all | bytes 1310720 | tf_op jit(solution)/shard_map/all_to_all | solution.py:15
  20.4 37.1 %all_to_all.31 = bf16[32,80,128]{2,1,0:T(8,128)(2,1)S(1)} all-to-all(bf16[32,80,128]{2,1,0:T(8,128)(2,1)S(1)} %bitcast.15), channel_id=1, replica_groups=mesh['chip'=8,'core'=2,'col'=32] {'col'}, dimensions={0} | all-to-all | bytes 1310720 | tf_op jit(solution)/shard_map/all_to_all | solution.py:15
  57.5 0.1 slice.16
  57.6 0.1 broadcast_in_dim.11
  57.7 0.1 pad_maximum_fusion.1
  57.8 21.9 %all_to_all.32 = bf16[8,768,128]{2,1,0:T(8,128)(2,1)S(1)} all-to-all(bf16[8,768,128]{2,1,0:T(8,128)(2,1)S(1)} %pad_maximum_fusion.1), channel_id=1, replica_groups=mesh['chip'=8,'core'=2,'col'=32] {'chip'}, dimensions={0} | all-to-all | bytes 3145728 | tf_op jit(solution)/shard_map/all_to_all | solution.py:15
  79.9 0.1 slice.19
  80.0 0.4 broadcast_in_dim.24
  80.4 0.2 pad_maximum_fusion
  80.6 5.8 %all_to_all.33.both_ref = bf16[2,8,640,128]{3,2,1,0:T(8,128)(2,1)S(1)} all-to-all(bf16[2,8,640,128]{3,2,1,0:T(8,128)(2,1)S(1)} %pad_maximum_fusion), channel_id=1, replica_groups=mesh['chip'=8,'core'=2,'col'=32] {'core'}, dimensions={0} | all-to-all | bytes 5242880 | tf_op jit(solution)/shard_map/all_to_all | solution.py:15
  86.4 1.3 shard_map.29
  87.7 26.4 %all_to_all.34 = bf16[32,32,256]{2,1,0:T(8,128)(2,1)S(1)} all-to-all(bf16[32,32,256]{2,1,0:T(8,128)(2,1)S(1)} %bitcast.14), channel_id=1, replica_groups=mesh['chip'=8,'core'=2,'col'=32] {'col'}, dimensions={0} | all-to-all | bytes 1048576 | tf_op jit(solution)/shard_map/all_to_all | solution.py:15
  114.2 0.1 reduce_sum.12
  114.2 0.1 broadcast_in_dim.25
  114.3 24.0 %all_to_all.35 = bf16[32,32,256]{2,1,0:T(8,128)(2,1)S(1)} all-to-all(bf16[32,32,256]{2,1,0:T(8,128)(2,1)S(1)} %broadcast_in_dim.25), channel_id=1, replica_groups=mesh['chip'=8,'core'=2,'col'=32] {'col'}, dimensions={0} | all-to-all | bytes 1048576 | tf_op jit(solution)/shard_map/all_to_all | solution.py:15
  138.3 1.5 %shard_map.30 = bf16[8,256,128]{2,1,0:T(8,128)(2,1)} custom-call(bf16[1024,256]{1,0:T(8,128)(2,1)S(1)} %bitcast.13, bf16[2,8,640,128]{3,2,1,0:T(8,128)(2,1)S(1)} %all_to_all.33.both_ref), custom_call_target="tpu_custom_call" | custom-call | tf_op jit(solution)/shard_map/pallas_call | solution.py:78
  (3 shorter events, 0.1 us)
Async XLA Ops:
  0.0 1.0 copy-start
  1.0 0.9 copy-start.1

commit v7 on v6

v7 whole, which is shorter than its diff:
```python
import jax
import jax.numpy as jnp
from jax import lax
from jax.experimental import pallas as pl
from jax.experimental.pallas import tpu as pltpu
from jax.sharding import Mesh, PartitionSpec as P

F32 = jnp.float32
BF16 = jnp.bfloat16
ROW = ("chip", "core")
VMEM = pl.BlockSpec(memory_space=pltpu.VMEM)
HBM = pl.BlockSpec(memory_space=pltpu.HBM)


def exchange(value, axes):
    return lax.all_to_all(value, axes, 0, 0, tiled=True)


def fit_kernel(both_ref, t_ref, out_ref):
    _, nj, block_a, block_b = t_ref.shape
    half = block_b // 2
    aux_half = both_ref.shape[2] - block_b
    straight = jnp.concatenate([t_ref[0, j] for j in range(nj)], axis=1)
    columns = []
    for side in range(2):
        rows = pl.ds(side * half, half)
        columns.append(
            jnp.concatenate([both_ref[s, j, rows, :] for j in range(nj) for s in range(2)], axis=0)
        )
    swapped = jnp.concatenate(columns, axis=1)
    for s in range(2):
        held = jnp.concatenate(
            [both_ref[s, j, pl.ds(block_b, aux_half), :] for j in range(nj)], axis=1
        )
        direct = lax.dot_general(
            held, straight, (((1,), (1,)), ((), ())), preferred_element_type=F32
        )
        mirror = jnp.dot(held, swapped, preferred_element_type=F32)
        out_ref[pl.ds(s * aux_half, aux_half), :] = (2.0 * direct - mirror).astype(BF16)


def pack_kernel(t_hbm, f_hbm, out_ref, t_ref, f_ref, sems):
    _, nj, _, block_b = t_ref.shape
    half = block_b // 2
    few = f_ref.shape[0] // 2
    load_f = pltpu.make_async_copy(f_hbm, f_ref, sems.at[0])
    load_t = pltpu.make_async_copy(t_hbm, t_ref, sems.at[1])
    load_f.start()
    load_t.start()
    load_f.wait()
    for bit in range(2):
        for side in range(2):
            piece = f_ref[pl.ds(bit * few, few), :, pl.ds(side * block_b, block_b)]
            by_j = jnp.swapaxes(piece.astype(F32), 0, 1).astype(BF16)
            for j in range(nj):
                out_ref[2 * j + bit, side, pl.ds(half, few), :] = by_j[j]
    load_t.wait()
    for bit in range(2):
        for side in range(2):
            rows = pl.ds(side * block_b + bit * half, half)
            for j in range(nj):
                out_ref[2 * j + bit, side, pl.ds(0, half), :] = t_ref[0, j, rows, :]


def project_kernel(fitted_ref, both_ref, out_hbm, out_ref, sems):
    _, nj, _, block_b = out_ref.shape
    aux_half = fitted_ref.shape[0] // 2
    turned = fitted_ref[...].T
    stores = []
    for j in range(0, nj, 2):
        held = jnp.concatenate(
            [
                jnp.concatenate(
                    [both_ref[s, j + i, pl.ds(block_b, aux_half), :] for s in range(2)], axis=0
                )
                for i in range(2)
            ],
            axis=1,
        )
        total = jnp.dot(turned, held, preferred_element_type=F32).astype(BF16)
        for i in range(2):
            out_ref[0, j + i] = total[:, i * block_b : (i + 1) * block_b]
            store = pltpu.make_async_copy(out_ref.at[0, j + i], out_hbm.at[0, j + i], sems.at[j + i])
            store.start()
            stores.append(store)
    for store in stores:
        store.wait()


def call(kernel, shapes, operands, inside=VMEM, outside=VMEM, scratch=()):
    return pl.pallas_call(
        kernel,
        out_shape=[jax.ShapeDtypeStruct(shape, BF16) for shape in shapes],
        in_specs=[inside] * len(operands),
        out_specs=[outside] * len(shapes),
        scratch_shapes=scratch,
        compiler_params=pltpu.CompilerParams(vmem_limit_bytes=32 << 20),
    )(*operands)


def body(amplitudes, factors):
    cores = lax.axis_size("core")
    chips = lax.axis_size("chip")
    cols = lax.axis_size("col")
    rows = chips * cores
    _, nj, block_a, block_b = amplitudes.shape
    block_q = factors.shape[0]
    aux = block_q * cols
    half = block_b // 2
    few = block_q // 2

    both, kept = call(
        pack_kernel,
        [(rows, 2, half + few, block_b), amplitudes.shape],
        [pltpu.with_memory_space_constraint(x, pltpu.HBM) for x in (amplitudes, factors)],
        inside=HBM,
        scratch=[pltpu.VMEM(factors.shape, BF16), pltpu.SemaphoreType.DMA((2,))],
    )
    both = exchange(both, ROW)
    both = exchange(both.reshape(cols, half + few, block_b), "col")
    x, y = both[:, :half], both[:, half:]

    x = x.reshape(chips, 4 * half, block_b)
    y = jnp.broadcast_to(y.reshape(1, cols * few, block_b), (chips, cols * few, block_b))
    both = exchange(jnp.concatenate([x, y], axis=1), "chip")

    x = jnp.transpose(both[:, : 4 * half].reshape(nj, 2, block_b, block_b), (1, 0, 2, 3))
    y = jnp.broadcast_to(both[None, :, 4 * half :], (2, nj, aux // 2, block_b))
    both = exchange(jnp.concatenate([x, y], axis=2), "core")

    (partial,) = call(fit_kernel, [(aux, block_a)], [both, kept])

    parts = exchange(partial.reshape(cols, block_q, block_a), "col")
    shard = jnp.sum(parts.astype(F32), axis=0).astype(BF16)
    copies = jnp.broadcast_to(shard[None], (cols, block_q, block_a))
    fitted = exchange(copies, "col").reshape(aux, block_a)

    (result,) = call(
        project_kernel,
        [amplitudes.shape],
        [fitted, both],
        outside=HBM,
        scratch=[pltpu.VMEM(amplitudes.shape, BF16), pltpu.SemaphoreType.DMA((nj,))],
    )
    return result


def solution(mesh):
    rows, cols = mesh.devices.shape
    fine = Mesh(mesh.devices.reshape(rows // 2, 2, cols), ("chip", "core", "col"))
    placed = (P(None, None, ROW, "col"), P("col", None, ROW))
    return jax.shard_map(
        body, mesh=fine, in_specs=placed, out_specs=P(None, None, ROW, "col"), check_vma=False
    )
```

time: 140 us -> 139 us (level)
  local copies, waits for them, and re-layouts: 2.74 us -> 0.8 us
    unnamed x4 -> x0, local copies, waits for them, and re-layouts: 1.94 us -> none
where the time goes in v7:
time: 139 us
  blocking collectives  134 us (96%)
  Pallas kernels  3.92 us (3%)
    all_to_all x6, blocking collectives, exchange(): return lax.all_to_all(value, axes, 0, 0, tiled=True)  134 us
    pallas_call x3, Pallas kernels, call(): pl.pallas_call(kernel, out_shape=[jax.ShapeDtypeStruct(shape, BF16) for s...  3.92 us

profile of v7, /device:TPU:8, one launch (start us, length us, event | category | flops | bytes accessed | tf_op | source)
XLA Modules:
  0.0 138.9 jit_solution(3171556698549584913)
XLA Ops:
  0.0 1.2 shard_map.28
  1.2 18.4 %all_to_all.30 = bf16[16,2,80,128]{3,2,1,0:T(8,128)(2,1)S(1)} all-to-all(bf16[16,2,80,128]{3,2,1,0:T(8,128)(2,1)S(1)} %get-tuple-element.7), channel_id=1, replica_groups=mesh['chip'=8,'core'=2,'col'=32] {'chip','core'}, dimensions={0} | all-to-all | bytes 1310720 | tf_op jit(solution)/shard_map/all_to_all | solution.py:16
  19.5 37.1 %all_to_all.31 = bf16[32,80,128]{2,1,0:T(8,128)(2,1)S(1)} all-to-all(bf16[32,80,128]{2,1,0:T(8,128)(2,1)S(1)} %bitcast.11), channel_id=1, replica_groups=mesh['chip'=8,'core'=2,'col'=32] {'col'}, dimensions={0} | all-to-all | bytes 1310720 | tf_op jit(solution)/shard_map/all_to_all | solution.py:16
  56.7 0.1 slice.16
  56.7 0.1 broadcast_in_dim.9
  56.9 0.1 pad_maximum_fusion.1
  57.0 21.9 %all_to_all.32 = bf16[8,768,128]{2,1,0:T(8,128)(2,1)S(1)} all-to-all(bf16[8,768,128]{2,1,0:T(8,128)(2,1)S(1)} %pad_maximum_fusion.1), channel_id=1, replica_groups=mesh['chip'=8,'core'=2,'col'=32] {'chip'}, dimensions={0} | all-to-all | bytes 3145728 | tf_op jit(solution)/shard_map/all_to_all | solution.py:16
  79.0 0.1 slice.19
  79.1 0.4 broadcast_in_dim.10
  79.5 0.2 pad_maximum_fusion
  79.7 5.8 %all_to_all.33.both_ref = bf16[2,8,640,128]{3,2,1,0:T(8,128)(2,1)S(1)} all-to-all(bf16[2,8,640,128]{3,2,1,0:T(8,128)(2,1)S(1)} %pad_maximum_fusion), channel_id=1, replica_groups=mesh['chip'=8,'core'=2,'col'=32] {'core'}, dimensions={0} | all-to-all | bytes 5242880 | tf_op jit(solution)/shard_map/all_to_all | solution.py:16
  85.6 1.3 shard_map.29
  86.8 26.4 %all_to_all.34 = bf16[32,32,256]{2,1,0:T(8,128)(2,1)S(1)} all-to-all(bf16[32,32,256]{2,1,0:T(8,128)(2,1)S(1)} %bitcast.10), channel_id=1, replica_groups=mesh['chip'=8,'core'=2,'col'=32] {'col'}, dimensions={0} | all-to-all | bytes 1048576 | tf_op jit(solution)/shard_map/all_to_all | solution.py:16
  113.3 0.1 reduce_sum.12
  113.4 0.1 broadcast_in_dim.22
  113.4 24.0 %all_to_all.35 = bf16[32,32,256]{2,1,0:T(8,128)(2,1)S(1)} all-to-all(bf16[32,32,256]{2,1,0:T(8,128)(2,1)S(1)} %broadcast_in_dim.22), channel_id=1, replica_groups=mesh['chip'=8,'core'=2,'col'=32] {'col'}, dimensions={0} | all-to-all | bytes 1048576 | tf_op jit(solution)/shard_map/all_to_all | solution.py:16
  137.4 1.5 %shard_map.30 = bf16[1,8,256,128]{3,2,1,0:T(8,128)(2,1)} custom-call(bf16[1024,256]{1,0:T(8,128)(2,1)S(1)} %bitcast.9, bf16[2,8,640,128]{3,2,1,0:T(8,128)(2,1)S(1)} %all_to_all.33.both_ref), custom_call_target="tpu_custom_call" | custom-call | tf_op jit(solution)/shard_map/pallas_call | solution.py:91
  (3 shorter events, 0.1 us)

commit v8 on v7

--- a/solution.py
+++ b/solution.py
@@ -16,22 +16,32 @@
     return lax.all_to_all(value, axes, 0, 0, tiled=True)
 
 
-def fit_kernel(both_ref, t_ref, out_ref):
+def places(core, block_b, aux_half):
+    own_t = pl.multiple_of(core * (block_b + aux_half), block_b)
+    other_t = pl.multiple_of(core * aux_half, block_b)
+    other_f = pl.multiple_of((1 - core) * block_b, block_b)
+    return own_t, other_t, other_f
+
+
+def fit_kernel(own_ref, other_ref, t_ref, out_ref):
     _, nj, block_a, block_b = t_ref.shape
     half = block_b // 2
-    aux_half = both_ref.shape[2] - block_b
+    aux_half = out_ref.shape[0] // 2
+    core = lax.axis_index("core")
+    own_t, other_t, other_f = places(core, block_b, aux_half)
     straight = jnp.concatenate([t_ref[0, j] for j in range(nj)], axis=1)
     columns = []
     for side in range(2):
-        rows = pl.ds(side * half, half)
-        columns.append(
-            jnp.concatenate([both_ref[s, j, rows, :] for j in range(nj) for s in range(2)], axis=0)
-        )
+        blocks = []
+        for j in range(nj):
+            mine = own_ref[j, pl.ds(own_t + side * half, half), :]
+            theirs = other_ref[j, pl.ds(other_t + side * half, half), :]
+            blocks.append(jnp.where(core == 0, mine, theirs))
+            blocks.append(jnp.where(core == 0, theirs, mine))
+        columns.append(jnp.concatenate(blocks, axis=0))
     swapped = jnp.concatenate(columns, axis=1)
-    for s in range(2):
-        held = jnp.concatenate(
-            [both_ref[s, j, pl.ds(block_b, aux_half), :] for j in range(nj)], axis=1
-        )
+    for s, (ref, start) in enumerate(((own_ref, block_b), (other_ref, other_f))):
+        held = jnp.concatenate([ref[j, pl.ds(start, aux_half), :] for j in range(nj)], axis=1)
         direct = lax.dot_general(
             held, straight, (((1,), (1,)), ((), ())), preferred_element_type=F32
         )
@@ -62,16 +72,21 @@
                 out_ref[2 * j + bit, side, pl.ds(0, half), :] = t_ref[0, j, rows, :]
 
 
-def project_kernel(fitted_ref, both_ref, out_hbm, out_ref, sems):
+def project_kernel(fitted_ref, own_ref, other_ref, out_hbm, out_ref, sems):
     _, nj, _, block_b = out_ref.shape
     aux_half = fitted_ref.shape[0] // 2
+    _, _, other_f = places(lax.axis_index("core"), block_b, aux_half)
     turned = fitted_ref[...].T
     stores = []
     for j in range(0, nj, 2):
         held = jnp.concatenate(
             [
                 jnp.concatenate(
-                    [both_ref[s, j + i, pl.ds(block_b, aux_half), :] for s in range(2)], axis=0
+                    [
+                        own_ref[j + i, pl.ds(block_b, aux_half), :],
+                        other_ref[j + i, pl.ds(other_f, aux_half), :],
+                    ],
+                    axis=0,
                 )
                 for i in range(2)
             ],
@@ -116,19 +131,21 @@
         inside=HBM,
         scratch=[pltpu.VMEM(factors.shape, BF16), pltpu.SemaphoreType.DMA((2,))],
     )
+    start = ((1 - lax.axis_index("core")) * block_b).astype(jnp.uint32)
+    both, start = lax.optimization_barrier((both, start))
     both = exchange(both, ROW)
     both = exchange(both.reshape(cols, half + few, block_b), "col")
     x, y = both[:, :half], both[:, half:]
 
-    x = x.reshape(chips, 4 * half, block_b)
+    x = x.reshape(chips, 2, block_b, block_b)
     y = jnp.broadcast_to(y.reshape(1, cols * few, block_b), (chips, cols * few, block_b))
-    both = exchange(jnp.concatenate([x, y], axis=1), "chip")
+    own = exchange(jnp.concatenate([x[:, 0], y, x[:, 1]], axis=1), "chip")
 
-    x = jnp.transpose(both[:, : 4 * half].reshape(nj, 2, block_b, block_b), (1, 0, 2, 3))
-    y = jnp.broadcast_to(both[None, :, 4 * half :], (2, nj, aux // 2, block_b))
-    both = exchange(jnp.concatenate([x, y], axis=2), "core")
+    zero = jnp.uint32(0)
+    other = lax.dynamic_slice(own, (zero, start, zero), (chips, block_b + aux // 2, block_b))
+    other = lax.ppermute(other, "core", [(0, 1), (1, 0)])
 
-    (partial,) = call(fit_kernel, [(aux, block_a)], [both, kept])
+    (partial,) = call(fit_kernel, [(aux, block_a)], [own, other, kept])
 
     parts = exchange(partial.reshape(cols, block_q, block_a), "col")
     shard = jnp.sum(parts.astype(F32), axis=0).astype(BF16)
@@ -138,7 +155,7 @@
     (result,) = call(
         project_kernel,
         [amplitudes.shape],
-        [fitted, both],
+        [fitted, own, other],
         outside=HBM,
         scratch=[pltpu.VMEM(amplitudes.shape, BF16), pltpu.SemaphoreType.DMA((nj,))],
     )

time: 139 us -> 138 us (level)
  blocking collectives: 134 us -> 128 us
  waiting for transfers between devices: 0 us -> 3 us
  starting transfers between devices: 0 us -> 1.92 us
    all_to_all x6 -> x5, blocking collectives: 134 us -> 128 us  [exchange(): return lax.all_to_all(value, axes, 0, 0, tiled=True)]
    ppermute x0 -> x1, waiting for transfers between devices: none -> 3 us  [body(): other = lax.ppermute(other, 'core', [(0, 1), (1, 0)])]
    ppermute x0 -> x1, starting transfers between devices: none -> 1.92 us  [body(): other = lax.ppermute(other, 'core', [(0, 1), (1, 0)])]
  transfers between devices with their start and end apart: 0 -> 1, of which waited for: 0 -> 1; matrix products, arithmetic and copies ran while one was open for 0% -> 0% of each run, Pallas kernels for 0% -> 0%
where the time goes in v8:
time: 138 us
  blocking collectives  128 us (93%)
  Pallas kernels  3.94 us (3%)
  waiting for transfers between devices  3 us (2%)
  starting transfers between devices  1.92 us (1%)
    all_to_all x5, blocking collectives, exchange(): return lax.all_to_all(value, axes, 0, 0, tiled=True)  128 us
    pallas_call x3, Pallas kernels, call(): pl.pallas_call(kernel, out_shape=[jax.ShapeDtypeStruct(shape, BF16) for s...  3.94 us
    ppermute x1, waiting for transfers between devices, body(): other = lax.ppermute(other, 'core', [(0, 1), (1, 0)])  3 us
  transfers between devices with their start and end apart: 1, of which 1 were waited for; matrix products, arithmetic and copies ran while one was open for 0% of the time, Pallas kernels for 0%

profile of v8, /device:TPU:8, one launch (start us, length us, event | category | flops | bytes accessed | tf_op | source)
XLA Modules:
  0.0 137.6 jit_solution(7505871961129921072)
XLA Ops:
  0.0 1.2 shard_map.28
  1.2 18.4 %all_to_all.25 = bf16[16,2,80,128]{3,2,1,0:T(8,128)(2,1)S(1)} all-to-all(bf16[16,2,80,128]{3,2,1,0:T(8,128)(2,1)S(1)} %get-tuple-element.10), channel_id=1, replica_groups=mesh['chip'=8,'core'=2,'col'=32] {'chip','core'}, dimensions={0} | all-to-all | bytes 1310720 | tf_op jit(solution)/shard_map/all_to_all | solution.py:16
  19.5 37.1 %all_to_all.26 = bf16[32,80,128]{2,1,0:T(8,128)(2,1)S(1)} all-to-all(bf16[32,80,128]{2,1,0:T(8,128)(2,1)S(1)} %bitcast.15), channel_id=1, replica_groups=mesh['chip'=8,'core'=2,'col'=32] {'col'}, dimensions={0} | all-to-all | bytes 1310720 | tf_op jit(solution)/shard_map/all_to_all | solution.py:16
  56.6 0.1 slice.16
  56.8 0.1 broadcast_in_dim.14
  56.9 0.1 pad_maximum_fusion
  57.0 21.9 %all_to_all.27.own_ref = bf16[8,768,128]{2,1,0:T(8,128)(2,1)S(1)} all-to-all(bf16[8,768,128]{2,1,0:T(8,128)(2,1)S(1)} %pad_maximum_fusion), channel_id=1, replica_groups=mesh['chip'=8,'core'=2,'col'=32] {'chip'}, dimensions={0} | all-to-all | bytes 3145728 | tf_op jit(solution)/shard_map/all_to_all | solution.py:16
  79.0 0.3 constant_dynamic-slice_fusion
  79.3 1.9 %collective-permute-start = (bf16[8,640,128]{2,1,0:T(8,128)(2,1)S(1)}, bf16[8,640,128]{2,1,0:T(8,128)(2,1)S(1)}, u32[]{:S(2)}, u32[]{:S(2)}) collective-permute-start(bf16[8,640,128]{2,1,0:T(8,128)(2,1)S(1)} %constant_dynamic-slice_fusion), channel_id=1, source_target_pairs={{0,32},{32,0},{1,33},{33,1},{2,34},{34,2},{3,35},{35,3},{4,36},{36... | collective-permute-start | bytes 3932168 | tf_op jit(solution)/shard_map/ppermute | solution.py:146
  81.2 3.0 %collective-permute-done.other_ref = bf16[8,640,128]{2,1,0:T(8,128)(2,1)S(1)} collective-permute-done((bf16[8,640,128]{2,1,0:T(8,128)(2,1)S(1)}, bf16[8,640,128]{2,1,0:T(8,128)(2,1)S(1)}, u32[]{:S(2)}, u32[]{:S(2)}) %collective-permute-start) | collective-permute-done | bytes 1310752 | tf_op jit(solution)/shard_map/ppermute | solution.py:146
  84.2 1.3 shard_map.29
  85.5 26.4 %all_to_all.28 = bf16[32,32,256]{2,1,0:T(8,128)(2,1)S(1)} all-to-all(bf16[32,32,256]{2,1,0:T(8,128)(2,1)S(1)} %bitcast.14), channel_id=1, replica_groups=mesh['chip'=8,'core'=2,'col'=32] {'col'}, dimensions={0} | all-to-all | bytes 1048576 | tf_op jit(solution)/shard_map/all_to_all | solution.py:16
  112.0 0.1 reduce_sum.12
  112.1 0.1 broadcast_in_dim.15
  112.1 24.0 %all_to_all.29 = bf16[32,32,256]{2,1,0:T(8,128)(2,1)S(1)} all-to-all(bf16[32,32,256]{2,1,0:T(8,128)(2,1)S(1)} %broadcast_in_dim.15), channel_id=1, replica_groups=mesh['chip'=8,'core'=2,'col'=32] {'col'}, dimensions={0} | all-to-all | bytes 1048576 | tf_op jit(solution)/shard_map/all_to_all | solution.py:16
  136.1 1.5 %shard_map.30 = bf16[1,8,256,128]{3,2,1,0:T(8,128)(2,1)} custom-call(bf16[1024,256]{1,0:T(8,128)(2,1)S(1)} %bitcast.13, bf16[8,768,128]{2,1,0:T(8,128)(2,1)S(1)} %all_to_all.27.own_ref, bf16[8,640,128]{2,1,0:T(8,128)(2,1)S(1)} %collective-permute-done.other_ref), custom_call_target="tpu_custom_call" | custom-call | tf_op jit(solution)/shard_map/pallas_call | solution.py:106
  (2 shorter events, 0.0 us)
Async XLA Ops:
  79.3 4.9 %collective-permute-start = (bf16[8,640,128]{2,1,0:T(8,128)(2,1)S(1)}, bf16[8,640,128]{2,1,0:T(8,128)(2,1)S(1)}, u32[]{:S(2)}, u32[]{:S(2)}) collective-permute-start(bf16[8,640,128]{2,1,0:T(8,128)(2,1)S(1)} %constant_dynamic-slice_fusion), channel_id=1, source_target_pairs={{0,32},{32,0},{1,33},{33,1},{2,34},{34,2},{3,35},{35,3},{4,36},{36... | collective-permute-start | bytes 3932168 | tf_op jit(solution)/shard_map/ppermute | solution.py:146

commit v9 on v8

--- a/solution.py
+++ b/solution.py
@@ -23,13 +23,22 @@
     return own_t, other_t, other_f
 
 
-def fit_kernel(own_ref, other_ref, t_ref, out_ref):
+def early_kernel(own_ref, t_ref, out_ref):
+    _, nj, _, block_b = t_ref.shape
+    aux_half = out_ref.shape[0]
+    held = jnp.concatenate([own_ref[j, pl.ds(block_b, aux_half), :] for j in range(nj)], axis=1)
+    straight = jnp.concatenate([t_ref[0, j] for j in range(nj)], axis=1)
+    out_ref[...] = 2.0 * lax.dot_general(
+        held, straight, (((1,), (1,)), ((), ())), preferred_element_type=F32
+    )
+
+
+def fit_kernel(own_ref, other_ref, t_ref, early_ref, out_ref):
     _, nj, block_a, block_b = t_ref.shape
     half = block_b // 2
     aux_half = out_ref.shape[0] // 2
     core = lax.axis_index("core")
     own_t, other_t, other_f = places(core, block_b, aux_half)
-    straight = jnp.concatenate([t_ref[0, j] for j in range(nj)], axis=1)
     columns = []
     for side in range(2):
         blocks = []
@@ -40,13 +49,16 @@
             blocks.append(jnp.where(core == 0, theirs, mine))
         columns.append(jnp.concatenate(blocks, axis=0))
     swapped = jnp.concatenate(columns, axis=1)
-    for s, (ref, start) in enumerate(((own_ref, block_b), (other_ref, other_f))):
-        held = jnp.concatenate([ref[j, pl.ds(start, aux_half), :] for j in range(nj)], axis=1)
-        direct = lax.dot_general(
-            held, straight, (((1,), (1,)), ((), ())), preferred_element_type=F32
-        )
-        mirror = jnp.dot(held, swapped, preferred_element_type=F32)
-        out_ref[pl.ds(s * aux_half, aux_half), :] = (2.0 * direct - mirror).astype(BF16)
+    held = jnp.concatenate([own_ref[j, pl.ds(block_b, aux_half), :] for j in range(nj)], axis=1)
+    mirror = jnp.dot(held, swapped, preferred_element_type=F32)
+    out_ref[pl.ds(0, aux_half), :] = (early_ref[...] - mirror).astype(BF16)
+    held = jnp.concatenate([other_ref[j, pl.ds(other_f, aux_half), :] for j in range(nj)], axis=1)
+    straight = jnp.concatenate([t_ref[0, j] for j in range(nj)], axis=1)
+    direct = lax.dot_general(
+        held, straight, (((1,), (1,)), ((), ())), preferred_element_type=F32
+    )
+    mirror = jnp.dot(held, swapped, preferred_element_type=F32)
+    out_ref[pl.ds(aux_half, aux_half), :] = (2.0 * direct - mirror).astype(BF16)
 
 
 def pack_kernel(t_hbm, f_hbm, out_ref, t_ref, f_ref, sems):
@@ -102,10 +114,10 @@
         store.wait()
 
 
-def call(kernel, shapes, operands, inside=VMEM, outside=VMEM, scratch=()):
+def call(kernel, shapes, operands, inside=VMEM, outside=VMEM, scratch=(), dtype=BF16):
     return pl.pallas_call(
         kernel,
-        out_shape=[jax.ShapeDtypeStruct(shape, BF16) for shape in shapes],
+        out_shape=[jax.ShapeDtypeStruct(shape, dtype) for shape in shapes],
         in_specs=[inside] * len(operands),
         out_specs=[outside] * len(shapes),
         scratch_shapes=scratch,
@@ -145,7 +157,8 @@
     other = lax.dynamic_slice(own, (zero, start, zero), (chips, block_b + aux // 2, block_b))
     other = lax.ppermute(other, "core", [(0, 1), (1, 0)])
 
-    (partial,) = call(fit_kernel, [(aux, block_a)], [own, other, kept])
+    (early,) = call(early_kernel, [(aux // 2, block_a)], [own, kept], dtype=F32)
+    (partial,) = call(fit_kernel, [(aux, block_a)], [own, other, kept, early])
 
     parts = exchange(partial.reshape(cols, block_q, block_a), "col")
     shard = jnp.sum(parts.astype(F32), axis=0).astype(BF16)

time: 138 us -> 138 us (level)
    pallas_call x3 -> x4, Pallas kernels: 3.94 us -> 4.13 us  [call(): pl.pallas_call(kernel, out_shape=[jax.ShapeDtypeStruct(shape, dtype) for...]
where the time goes in v9:
time: 138 us; the launch traced here: 137 us
  blocking collectives  128 us (93%)
  Pallas kernels  4.13 us (3%)
  waiting for transfers between devices  2.52 us (2%)
  starting transfers between devices  1.92 us (1%)
    all_to_all x5, blocking collectives, exchange(): return lax.all_to_all(value, axes, 0, 0, tiled=True)  128 us
    pallas_call x4, Pallas kernels, call(): pl.pallas_call(kernel, out_shape=[jax.ShapeDtypeStruct(shape, dtype) for...  4.13 us
  transfers between devices with their start and end apart: 1, of which 1 were waited for; matrix products, arithmetic and copies ran while one was open for 0% of the time, Pallas kernels for 0%

profile of v9, /device:TPU:8, one launch (start us, length us, event | category | flops | bytes accessed | tf_op | source)
XLA Modules:
  0.0 137.3 jit_solution(4731762605911046744)
XLA Ops:
  0.0 1.2 shard_map.28
  1.2 18.4 %all_to_all.25 = bf16[16,2,80,128]{3,2,1,0:T(8,128)(2,1)S(1)} all-to-all(bf16[16,2,80,128]{3,2,1,0:T(8,128)(2,1)S(1)} %get-tuple-element.10), channel_id=1, replica_groups=mesh['chip'=8,'core'=2,'col'=32] {'chip','core'}, dimensions={0} | all-to-all | bytes 1310720 | tf_op jit(solution)/shard_map/all_to_all | solution.py:16
  19.5 37.1 %all_to_all.26 = bf16[32,80,128]{2,1,0:T(8,128)(2,1)S(1)} all-to-all(bf16[32,80,128]{2,1,0:T(8,128)(2,1)S(1)} %bitcast.15), channel_id=1, replica_groups=mesh['chip'=8,'core'=2,'col'=32] {'col'}, dimensions={0} | all-to-all | bytes 1310720 | tf_op jit(solution)/shard_map/all_to_all | solution.py:16
  56.6 0.1 slice.16
  56.8 0.1 broadcast_in_dim.14
  56.9 0.1 pad_maximum_fusion
  57.0 21.9 %all_to_all.27.own_ref = bf16[8,768,128]{2,1,0:T(8,128)(2,1)S(1)} all-to-all(bf16[8,768,128]{2,1,0:T(8,128)(2,1)S(1)} %pad_maximum_fusion), channel_id=1, replica_groups=mesh['chip'=8,'core'=2,'col'=32] {'chip'}, dimensions={0} | all-to-all | bytes 3145728 | tf_op jit(solution)/shard_map/all_to_all | solution.py:16
  79.0 0.3 constant_dynamic-slice_fusion
  79.3 1.9 %collective-permute-start = (bf16[8,640,128]{2,1,0:T(8,128)(2,1)S(1)}, bf16[8,640,128]{2,1,0:T(8,128)(2,1)S(1)}, u32[]{:S(2)}, u32[]{:S(2)}) collective-permute-start(bf16[8,640,128]{2,1,0:T(8,128)(2,1)S(1)} %constant_dynamic-slice_fusion), channel_id=1, source_target_pairs={{0,32},{32,0},{1,33},{33,1},{2,34},{34,2},{3,35},{35,3},{4,36},{36... | collective-permute-start | bytes 3932168 | tf_op jit(solution)/shard_map/ppermute | solution.py:158
  81.2 0.5 shard_map.29.early_ref
  81.7 2.5 %collective-permute-done.other_ref = bf16[8,640,128]{2,1,0:T(8,128)(2,1)S(1)} collective-permute-done((bf16[8,640,128]{2,1,0:T(8,128)(2,1)S(1)}, bf16[8,640,128]{2,1,0:T(8,128)(2,1)S(1)}, u32[]{:S(2)}, u32[]{:S(2)}) %collective-permute-start) | collective-permute-done | bytes 1310752 | tf_op jit(solution)/shard_map/ppermute | solution.py:158
  84.2 1.0 shard_map.30
  85.2 26.4 %all_to_all.28 = bf16[32,32,256]{2,1,0:T(8,128)(2,1)S(1)} all-to-all(bf16[32,32,256]{2,1,0:T(8,128)(2,1)S(1)} %bitcast.14), channel_id=1, replica_groups=mesh['chip'=8,'core'=2,'col'=32] {'col'}, dimensions={0} | all-to-all | bytes 1048576 | tf_op jit(solution)/shard_map/all_to_all | solution.py:16
  111.7 0.1 reduce_sum.12
  111.8 0.1 broadcast_in_dim.15
  111.8 24.0 %all_to_all.29 = bf16[32,32,256]{2,1,0:T(8,128)(2,1)S(1)} all-to-all(bf16[32,32,256]{2,1,0:T(8,128)(2,1)S(1)} %broadcast_in_dim.15), channel_id=1, replica_groups=mesh['chip'=8,'core'=2,'col'=32] {'col'}, dimensions={0} | all-to-all | bytes 1048576 | tf_op jit(solution)/shard_map/all_to_all | solution.py:16
  135.8 1.5 %shard_map.31 = bf16[1,8,256,128]{3,2,1,0:T(8,128)(2,1)} custom-call(bf16[1024,256]{1,0:T(8,128)(2,1)S(1)} %bitcast.13, bf16[8,768,128]{2,1,0:T(8,128)(2,1)S(1)} %all_to_all.27.own_ref, bf16[8,640,128]{2,1,0:T(8,128)(2,1)S(1)} %collective-permute-done.other_ref), custom_call_target="tpu_custom_call" | custom-call | tf_op jit(solution)/shard_map/pallas_call | solution.py:118
  (2 shorter events, 0.0 us)
Async XLA Ops:
  79.3 4.9 %collective-permute-start = (bf16[8,640,128]{2,1,0:T(8,128)(2,1)S(1)}, bf16[8,640,128]{2,1,0:T(8,128)(2,1)S(1)}, u32[]{:S(2)}, u32[]{:S(2)}) collective-permute-start(bf16[8,640,128]{2,1,0:T(8,128)(2,1)S(1)} %constant_dynamic-slice_fusion), channel_id=1, source_target_pairs={{0,32},{32,0},{1,33},{33,1},{2,34},{34,2},{3,35},{35,3},{4,36},{36... | collective-permute-start | bytes 3932168 | tf_op jit(solution)/shard_map/ppermute | solution.py:158

commit v10 on v7

--- a/solution.py
+++ b/solution.py
@@ -16,27 +16,41 @@
     return lax.all_to_all(value, axes, 0, 0, tiled=True)
 
 
-def fit_kernel(both_ref, t_ref, out_ref):
-    _, nj, block_a, block_b = t_ref.shape
+def product(factors_of, own_ref, t_ref):
+    _, nj, _, block_b = t_ref.shape
     half = block_b // 2
-    aux_half = both_ref.shape[2] - block_b
+    held = jnp.concatenate([factors_of(j) for j in range(nj)], axis=1)
     straight = jnp.concatenate([t_ref[0, j] for j in range(nj)], axis=1)
-    columns = []
-    for side in range(2):
-        rows = pl.ds(side * half, half)
-        columns.append(
-            jnp.concatenate([both_ref[s, j, rows, :] for j in range(nj) for s in range(2)], axis=0)
-        )
-    swapped = jnp.concatenate(columns, axis=1)
-    for s in range(2):
-        held = jnp.concatenate(
-            [both_ref[s, j, pl.ds(block_b, aux_half), :] for j in range(nj)], axis=1
-        )
-        direct = lax.dot_general(
-            held, straight, (((1,), (1,)), ((), ())), preferred_element_type=F32
-        )
-        mirror = jnp.dot(held, swapped, preferred_element_type=F32)
-        out_ref[pl.ds(s * aux_half, aux_half), :] = (2.0 * direct - mirror).astype(BF16)
+    swapped = jnp.concatenate(
+        [
+            jnp.concatenate(
+                [own_ref[i, pl.ds(side * half, half), :] for i in range(2 * nj)], axis=0
+            )
+            for side in range(2)
+        ],
+        axis=1,
+    )
+    direct = lax.dot_general(
+        held, straight, (((1,), (1,)), ((), ())), preferred_element_type=F32
+    )
+    mirror = jnp.dot(held, swapped, preferred_element_type=F32)
+    return (2.0 * direct - mirror).astype(BF16)
+
+
+def rows_of(ref, j, start):
+    size = ref.shape[1] - start
+    return jnp.concatenate([ref[2 * j + i, pl.ds(start, size), :] for i in range(2)], axis=0)
+
+
+def early_kernel(own_ref, t_ref, out_ref):
+    start = t_ref.shape[3]
+    out_ref[...] = product(lambda j: rows_of(own_ref, j, start), own_ref, t_ref)
+
+
+def late_kernel(own_ref, other_ref, t_ref, early_ref, out_ref):
+    count = early_ref.shape[0]
+    out_ref[pl.ds(0, count), :] = early_ref[...]
+    out_ref[pl.ds(count, count), :] = product(lambda j: rows_of(other_ref, j, 0), own_ref, t_ref)
 
 
 def pack_kernel(t_hbm, f_hbm, out_ref, t_ref, f_ref, sems):
@@ -62,16 +76,15 @@
                 out_ref[2 * j + bit, side, pl.ds(0, half), :] = t_ref[0, j, rows, :]
 
 
-def project_kernel(fitted_ref, both_ref, out_hbm, out_ref, sems):
+def project_kernel(fitted_ref, own_ref, other_ref, out_hbm, out_ref, sems):
     _, nj, _, block_b = out_ref.shape
-    aux_half = fitted_ref.shape[0] // 2
     turned = fitted_ref[...].T
     stores = []
     for j in range(0, nj, 2):
         held = jnp.concatenate(
             [
                 jnp.concatenate(
-                    [both_ref[s, j + i, pl.ds(block_b, aux_half), :] for s in range(2)], axis=0
+                    [rows_of(own_ref, j + i, block_b), rows_of(other_ref, j + i, 0)], axis=0
                 )
                 for i in range(2)
             ],
@@ -120,15 +133,15 @@
     both = exchange(both.reshape(cols, half + few, block_b), "col")
     x, y = both[:, :half], both[:, half:]
 
-    x = x.reshape(chips, 4 * half, block_b)
-    y = jnp.broadcast_to(y.reshape(1, cols * few, block_b), (chips, cols * few, block_b))
-    both = exchange(jnp.concatenate([x, y], axis=1), "chip")
+    x = x.reshape(rows, block_b, block_b)
+    y = y.reshape(1, cores, aux // 4, block_b)
+    y = jnp.broadcast_to(y, (chips, cores, aux // 4, block_b)).reshape(rows, aux // 4, block_b)
+    own = exchange(jnp.concatenate([x, y], axis=1), ROW)
 
-    x = jnp.transpose(both[:, : 4 * half].reshape(nj, 2, block_b, block_b), (1, 0, 2, 3))
-    y = jnp.broadcast_to(both[None, :, 4 * half :], (2, nj, aux // 2, block_b))
-    both = exchange(jnp.concatenate([x, y], axis=2), "core")
+    other = lax.ppermute(own[:, block_b:], "core", [(0, 1), (1, 0)])
 
-    (partial,) = call(fit_kernel, [(aux, block_a)], [both, kept])
+    (early,) = call(early_kernel, [(aux // 2, block_a)], [own, kept])
+    (partial,) = call(late_kernel, [(aux, block_a)], [own, other, kept, early])
 
     parts = exchange(partial.reshape(cols, block_q, block_a), "col")
     shard = jnp.sum(parts.astype(F32), axis=0).astype(BF16)
@@ -138,7 +151,7 @@
     (result,) = call(
         project_kernel,
         [amplitudes.shape],
-        [fitted, both],
+        [fitted, own, other],
         outside=HBM,
         scratch=[pltpu.VMEM(amplitudes.shape, BF16), pltpu.SemaphoreType.DMA((nj,))],
     )

time: 139 us -> 138 us (level)
  blocking collectives: 134 us -> 129 us
  starting transfers between devices: 0 us -> 1.92 us
  waiting for transfers between devices: 0 us -> 1.89 us
    all_to_all x6 -> x5, blocking collectives: 134 us -> 129 us  [exchange(): return lax.all_to_all(value, axes, 0, 0, tiled=True)]
    ppermute x0 -> x1, starting transfers between devices: none -> 1.92 us  [body(): other = lax.ppermute(own[:, block_b:], 'core', [(0, 1), (1, 0)])]
    ppermute x0 -> x1, waiting for transfers between devices: none -> 1.89 us  [body(): other = lax.ppermute(own[:, block_b:], 'core', [(0, 1), (1, 0)])]
    pallas_call x3 -> x4, Pallas kernels: 3.92 us -> 4.12 us  [call(): pl.pallas_call(kernel, out_shape=[jax.ShapeDtypeStruct(shape, BF16) for s...]
  transfers between devices with their start and end apart: 0 -> 1, of which waited for: 0 -> 1; matrix products, arithmetic and copies ran while one was open for 0% -> 0% of each run, Pallas kernels for 0% -> 1%
where the time goes in v10:
time: 138 us
  blocking collectives  129 us (93%)
  Pallas kernels  4.12 us (3%)
  starting transfers between devices  1.92 us (1%)
  waiting for transfers between devices  1.89 us (1%)
    all_to_all x5, blocking collectives, exchange(): return lax.all_to_all(value, axes, 0, 0, tiled=True)  129 us
    pallas_call x4, Pallas kernels, call(): pl.pallas_call(kernel, out_shape=[jax.ShapeDtypeStruct(shape, BF16) for s...  4.12 us
  transfers between devices with their start and end apart: 1, of which 1 were waited for; matrix products, arithmetic and copies ran while one was open for 0% of the time, Pallas kernels for 1%

profile of v10, /device:TPU:8, one launch (start us, length us, event | category | flops | bytes accessed | tf_op | source)
XLA Modules:
  0.0 137.7 jit_solution(6078892317718326303)
XLA Ops:
  0.0 1.2 shard_map.28
  1.2 18.4 %all_to_all.25 = bf16[16,2,80,128]{3,2,1,0:T(8,128)(2,1)S(1)} all-to-all(bf16[16,2,80,128]{3,2,1,0:T(8,128)(2,1)S(1)} %get-tuple-element.7), channel_id=1, replica_groups=mesh['chip'=8,'core'=2,'col'=32] {'chip','core'}, dimensions={0} | all-to-all | bytes 1310720 | tf_op jit(solution)/shard_map/all_to_all | solution.py:16
  19.5 37.1 %all_to_all.26 = bf16[32,80,128]{2,1,0:T(8,128)(2,1)S(1)} all-to-all(bf16[32,80,128]{2,1,0:T(8,128)(2,1)S(1)} %bitcast.9), channel_id=1, replica_groups=mesh['chip'=8,'core'=2,'col'=32] {'col'}, dimensions={0} | all-to-all | bytes 1310720 | tf_op jit(solution)/shard_map/all_to_all | solution.py:16
  56.7 0.1 slice.12
  56.7 0.2 broadcast_in_dim.14
  56.9 0.1 pad_maximum_fusion
  57.1 24.7 %all_to_all.27.own_ref = bf16[16,384,128]{2,1,0:T(8,128)(2,1)S(1)} all-to-all(bf16[16,384,128]{2,1,0:T(8,128)(2,1)S(1)} %pad_maximum_fusion), channel_id=1, replica_groups=mesh['chip'=8,'core'=2,'col'=32] {'chip','core'}, dimensions={0} | all-to-all | bytes 3145728 | tf_op jit(solution)/shard_map/all_to_all | solution.py:16
  81.8 0.1 slice.14
  81.9 1.9 %collective-permute-start = (bf16[16,256,128]{2,1,0:T(8,128)(2,1)S(1)}, bf16[16,256,128]{2,1,0:T(8,128)(2,1)S(1)}, u32[]{:S(2)}, u32[]{:S(2)}) collective-permute-start(bf16[16,256,128]{2,1,0:T(8,128)(2,1)S(1)} %slice.14), channel_id=1, source_target_pairs={{0,32},{32,0},{1,33},{33,1},{2,34},{34,2},{3,35},{35,3},{4,36},{36... | collective-permute-start | bytes 3145736 | tf_op jit(solution)/shard_map/ppermute | solution.py:141
  83.8 0.7 shard_map.29.early_ref
  84.5 1.9 %collective-permute-done.other_ref = bf16[16,256,128]{2,1,0:T(8,128)(2,1)S(1)} collective-permute-done((bf16[16,256,128]{2,1,0:T(8,128)(2,1)S(1)}, bf16[16,256,128]{2,1,0:T(8,128)(2,1)S(1)}, u32[]{:S(2)}, u32[]{:S(2)}) %collective-permute-start) | collective-permute-done | bytes 1048608 | tf_op jit(solution)/shard_map/ppermute | solution.py:141
  86.4 0.7 shard_map.30
  87.2 24.8 %all_to_all.28 = bf16[32,32,256]{2,1,0:T(8,128)(2,1)S(1)} all-to-all(bf16[32,32,256]{2,1,0:T(8,128)(2,1)S(1)} %bitcast.7), channel_id=1, replica_groups=mesh['chip'=8,'core'=2,'col'=32] {'col'}, dimensions={0} | all-to-all | bytes 1048576 | tf_op jit(solution)/shard_map/all_to_all | solution.py:16
  112.0 0.1 reduce_sum.12
  112.1 0.1 broadcast_in_dim.15
  112.1 24.1 %all_to_all.29 = bf16[32,32,256]{2,1,0:T(8,128)(2,1)S(1)} all-to-all(bf16[32,32,256]{2,1,0:T(8,128)(2,1)S(1)} %broadcast_in_dim.15), channel_id=1, replica_groups=mesh['chip'=8,'core'=2,'col'=32] {'col'}, dimensions={0} | all-to-all | bytes 1048576 | tf_op jit(solution)/shard_map/all_to_all | solution.py:16
  136.2 1.5 %shard_map.31 = bf16[1,8,256,128]{3,2,1,0:T(8,128)(2,1)} custom-call(bf16[1024,256]{1,0:T(8,128)(2,1)S(1)} %bitcast.6, bf16[16,384,128]{2,1,0:T(8,128)(2,1)S(1)} %all_to_all.27.own_ref, bf16[16,256,128]{2,1,0:T(8,128)(2,1)S(1)} %collective-permute-done.other_ref), custom_call_target="tpu_custom_call" | custom-call | tf_op jit(solution)/shard_map/pallas_call | solution.py:104
  (1 shorter events, 0.0 us)
Async XLA Ops:
  81.9 4.6 %collective-permute-start = (bf16[16,256,128]{2,1,0:T(8,128)(2,1)S(1)}, bf16[16,256,128]{2,1,0:T(8,128)(2,1)S(1)}, u32[]{:S(2)}, u32[]{:S(2)}) collective-permute-start(bf16[16,256,128]{2,1,0:T(8,128)(2,1)S(1)} %slice.14), channel_id=1, source_target_pairs={{0,32},{32,0},{1,33},{33,1},{2,34},{34,2},{3,35},{35,3},{4,36},{36... | collective-permute-start | bytes 3145736 | tf_op jit(solution)/shard_map/ppermute | solution.py:141

commit v11 on v9

--- a/solution.py
+++ b/solution.py
@@ -82,6 +82,25 @@
             rows = pl.ds(side * block_b + bit * half, half)
             for j in range(nj):
                 out_ref[2 * j + bit, side, pl.ds(0, half), :] = t_ref[0, j, rows, :]
+
+
+def spread_kernel(both_ref, out_ref):
+    chips, _, block_b = out_ref.shape
+    half = block_b // 2
+    count = both_ref.shape[0]
+    per_chip = count // chips
+    few = both_ref.shape[1] - half
+    factors = both_ref[:, pl.ds(half, few), :].reshape(count * few, block_b)
+    for chip in range(chips):
+        out_ref[chip, pl.ds(block_b, count * few), :] = factors
+        for i in range(per_chip):
+            place = i * half + (i // 2) * count * few
+            out_ref[chip, pl.ds(place, half), :] = both_ref[chip * per_chip + i, pl.ds(0, half), :]
+
+
+def sum_kernel(parts_ref, out_ref):
+    total = jnp.sum(parts_ref[...].astype(F32), axis=0).astype(BF16)
+    out_ref[...] = jnp.broadcast_to(total[None], out_ref.shape)
 
 
 def project_kernel(fitted_ref, own_ref, other_ref, out_hbm, out_ref, sems):
@@ -147,11 +166,9 @@
     both, start = lax.optimization_barrier((both, start))
     both = exchange(both, ROW)
     both = exchange(both.reshape(cols, half + few, block_b), "col")
-    x, y = both[:, :half], both[:, half:]
-
-    x = x.reshape(chips, 2, block_b, block_b)
-    y = jnp.broadcast_to(y.reshape(1, cols * few, block_b), (chips, cols * few, block_b))
-    own = exchange(jnp.concatenate([x[:, 0], y, x[:, 1]], axis=1), "chip")
+
+    (both,) = call(spread_kernel, [(chips, 2 * block_b + aux // 2, block_b)], [both])
+    own = exchange(both, "chip")
 
     zero = jnp.uint32(0)
     other = lax.dynamic_slice(own, (zero, start, zero), (chips, block_b + aux // 2, block_b))
@@ -161,8 +178,7 @@
     (partial,) = call(fit_kernel, [(aux, block_a)], [own, other, kept, early])
 
     parts = exchange(partial.reshape(cols, block_q, block_a), "col")
-    shard = jnp.sum(parts.astype(F32), axis=0).astype(BF16)
-    copies = jnp.broadcast_to(shard[None], (cols, block_q, block_a))
+    (copies,) = call(sum_kernel, [parts.shape], [parts])
     fitted = exchange(copies, "col").reshape(aux, block_a)
 
     (result,) = call(

time: 138 us -> 137 us (level)
    pallas_call x4 -> x6, Pallas kernels: 4.13 us -> 4.41 us  [call(): pl.pallas_call(kernel, out_shape=[jax.ShapeDtypeStruct(shape, dtype) for...]
where the time goes in v11:
time: 137 us
  blocking collectives  128 us (93%)
  Pallas kernels  4.41 us (3%)
  waiting for transfers between devices  2.52 us (2%)
  starting transfers between devices  1.92 us (1%)
    all_to_all x5, blocking collectives, exchange(): return lax.all_to_all(value, axes, 0, 0, tiled=True)  128 us
    pallas_call x6, Pallas kernels, call(): pl.pallas_call(kernel, out_shape=[jax.ShapeDtypeStruct(shape, dtype) for...  4.41 us
  transfers between devices with their start and end apart: 1, of which 1 were waited for; matrix products, arithmetic and copies ran while one was open for 0% of the time, Pallas kernels for 0%

profile of v11, /device:TPU:8, one launch (start us, length us, event | category | flops | bytes accessed | tf_op | source)
XLA Modules:
  0.0 137.1 jit_solution(5348354172399570885)
XLA Ops:
  0.0 1.2 shard_map.28
  1.2 18.4 %all_to_all.25 = bf16[16,2,80,128]{3,2,1,0:T(8,128)(2,1)S(1)} all-to-all(bf16[16,2,80,128]{3,2,1,0:T(8,128)(2,1)S(1)} %get-tuple-element.10), channel_id=1, replica_groups=mesh['chip'=8,'core'=2,'col'=32] {'chip','core'}, dimensions={0} | all-to-all | bytes 1310720 | tf_op jit(solution)/shard_map/all_to_all | solution.py:16
  19.5 37.1 %all_to_all.26.both_ref = bf16[32,80,128]{2,1,0:T(8,128)(2,1)S(1)} all-to-all(bf16[32,80,128]{2,1,0:T(8,128)(2,1)S(1)} %bitcast.5), channel_id=1, replica_groups=mesh['chip'=8,'core'=2,'col'=32] {'col'}, dimensions={0} | all-to-all | bytes 1310720 | tf_op jit(solution)/shard_map/all_to_all | solution.py:16
  56.6 0.2 shard_map.29
  56.8 21.9 %all_to_all.27.own_ref = bf16[8,768,128]{2,1,0:T(8,128)(2,1)S(1)} all-to-all(bf16[8,768,128]{2,1,0:T(8,128)(2,1)S(1)} %shard_map.29), channel_id=1, replica_groups=mesh['chip'=8,'core'=2,'col'=32] {'chip'}, dimensions={0} | all-to-all | bytes 3145728 | tf_op jit(solution)/shard_map/all_to_all | solution.py:16
  78.8 0.3 constant_dynamic-slice_fusion
  79.1 1.9 %collective-permute-start = (bf16[8,640,128]{2,1,0:T(8,128)(2,1)S(1)}, bf16[8,640,128]{2,1,0:T(8,128)(2,1)S(1)}, u32[]{:S(2)}, u32[]{:S(2)}) collective-permute-start(bf16[8,640,128]{2,1,0:T(8,128)(2,1)S(1)} %constant_dynamic-slice_fusion), channel_id=1, source_target_pairs={{0,32},{32,0},{1,33},{33,1},{2,34},{34,2},{3,35},{35,3},{4,36},{36... | collective-permute-start | bytes 3932168 | tf_op jit(solution)/shard_map/ppermute | solution.py:175
  81.0 0.5 shard_map.30.early_ref
  81.5 2.5 %collective-permute-done.other_ref = bf16[8,640,128]{2,1,0:T(8,128)(2,1)S(1)} collective-permute-done((bf16[8,640,128]{2,1,0:T(8,128)(2,1)S(1)}, bf16[8,640,128]{2,1,0:T(8,128)(2,1)S(1)}, u32[]{:S(2)}, u32[]{:S(2)}) %collective-permute-start) | collective-permute-done | bytes 1310752 | tf_op jit(solution)/shard_map/ppermute | solution.py:175
  84.0 1.0 shard_map.31
  85.0 26.4 %all_to_all.28.parts_ref = bf16[32,32,256]{2,1,0:T(8,128)(2,1)S(1)} all-to-all(bf16[32,32,256]{2,1,0:T(8,128)(2,1)S(1)} %bitcast.4), channel_id=1, replica_groups=mesh['chip'=8,'core'=2,'col'=32] {'col'}, dimensions={0} | all-to-all | bytes 1048576 | tf_op jit(solution)/shard_map/all_to_all | solution.py:16
  111.5 0.1 shard_map.32
  111.6 24.0 %all_to_all.29 = bf16[32,32,256]{2,1,0:T(8,128)(2,1)S(1)} all-to-all(bf16[32,32,256]{2,1,0:T(8,128)(2,1)S(1)} %shard_map.32), channel_id=1, replica_groups=mesh['chip'=8,'core'=2,'col'=32] {'col'}, dimensions={0} | all-to-all | bytes 1048576 | tf_op jit(solution)/shard_map/all_to_all | solution.py:16
  135.6 1.5 %shard_map.33 = bf16[1,8,256,128]{3,2,1,0:T(8,128)(2,1)} custom-call(bf16[1024,256]{1,0:T(8,128)(2,1)S(1)} %bitcast.3, bf16[8,768,128]{2,1,0:T(8,128)(2,1)S(1)} %all_to_all.27.own_ref, bf16[8,640,128]{2,1,0:T(8,128)(2,1)S(1)} %collective-permute-done.other_ref), custom_call_target="tpu_custom_call" | custom-call | tf_op jit(solution)/shard_map/pallas_call | solution.py:137
Async XLA Ops:
  79.1 4.9 %collective-permute-start = (bf16[8,640,128]{2,1,0:T(8,128)(2,1)S(1)}, bf16[8,640,128]{2,1,0:T(8,128)(2,1)S(1)}, u32[]{:S(2)}, u32[]{:S(2)}) collective-permute-start(bf16[8,640,128]{2,1,0:T(8,128)(2,1)S(1)} %constant_dynamic-slice_fusion), channel_id=1, source_target_pairs={{0,32},{32,0},{1,33},{33,1},{2,34},{34,2},{3,35},{35,3},{4,36},{36... | collective-permute-start | bytes 3932168 | tf_op jit(solution)/shard_map/ppermute | solution.py:175

commit v12 on v9

--- a/solution.py
+++ b/solution.py
@@ -8,6 +8,7 @@
 F32 = jnp.float32
 BF16 = jnp.bfloat16
 ROW = ("chip", "core")
+COL = ("y", "z")
 VMEM = pl.BlockSpec(memory_space=pltpu.VMEM)
 HBM = pl.BlockSpec(memory_space=pltpu.HBM)
 
@@ -128,7 +129,8 @@
 def body(amplitudes, factors):
     cores = lax.axis_size("core")
     chips = lax.axis_size("chip")
-    cols = lax.axis_size("col")
+    along_y, along_z = lax.axis_size("y"), lax.axis_size("z")
+    cols = along_y * along_z
     rows = chips * cores
     _, nj, block_a, block_b = amplitudes.shape
     block_q = factors.shape[0]
@@ -146,7 +148,7 @@
     start = ((1 - lax.axis_index("core")) * block_b).astype(jnp.uint32)
     both, start = lax.optimization_barrier((both, start))
     both = exchange(both, ROW)
-    both = exchange(both.reshape(cols, half + few, block_b), "col")
+    both = exchange(both.reshape(cols, half + few, block_b), COL)
     x, y = both[:, :half], both[:, half:]
 
     x = x.reshape(chips, 2, block_b, block_b)
@@ -160,10 +162,12 @@
     (early,) = call(early_kernel, [(aux // 2, block_a)], [own, kept], dtype=F32)
     (partial,) = call(fit_kernel, [(aux, block_a)], [own, other, kept, early])
 
-    parts = exchange(partial.reshape(cols, block_q, block_a), "col")
+    parts = exchange(partial.reshape(cols, block_q, block_a), ("z", "y"))
     shard = jnp.sum(parts.astype(F32), axis=0).astype(BF16)
-    copies = jnp.broadcast_to(shard[None], (cols, block_q, block_a))
-    fitted = exchange(copies, "col").reshape(aux, block_a)
+    copies = jnp.broadcast_to(shard[None], (along_y, block_q, block_a))
+    some = exchange(copies, "y").reshape(1, along_y * block_q, block_a)
+    copies = jnp.broadcast_to(some, (along_z, along_y * block_q, block_a))
+    fitted = exchange(copies, "z").reshape(aux, block_a)
 
     (result,) = call(
         project_kernel,
@@ -177,8 +181,8 @@
 
 def solution(mesh):
     rows, cols = mesh.devices.shape
-    fine = Mesh(mesh.devices.reshape(rows // 2, 2, cols), ("chip", "core", "col"))
-    placed = (P(None, None, ROW, "col"), P("col", None, ROW))
+    fine = Mesh(mesh.devices.reshape(rows // 2, 2, cols // 4, 4), ROW + COL)
+    placed = (P(None, None, ROW, COL), P(COL, None, ROW))
     return jax.shard_map(
-        body, mesh=fine, in_specs=placed, out_specs=P(None, None, ROW, "col"), check_vma=False
+        body, mesh=fine, in_specs=placed, out_specs=P(None, None, ROW, COL), check_vma=False
     )

time: 138 us -> 143 us (1.036)
  blocking collectives: 128 us -> 133 us
    all_to_all x5 -> x6, blocking collectives: 128 us -> 133 us  [exchange(): return lax.all_to_all(value, axes, 0, 0, tiled=True)]
where the time goes in v12:
time: 143 us
  blocking collectives  133 us (93%)
  Pallas kernels  4.13 us (3%)
  waiting for transfers between devices  2.52 us (2%)
  starting transfers between devices  1.92 us (1%)
    all_to_all x6, blocking collectives, exchange(): return lax.all_to_all(value, axes, 0, 0, tiled=True)  133 us
    pallas_call x4, Pallas kernels, call(): pl.pallas_call(kernel, out_shape=[jax.ShapeDtypeStruct(shape, dtype) for...  4.13 us
  transfers between devices with their start and end apart: 1, of which 1 were waited for; matrix products, arithmetic and copies ran while one was open for 0% of the time, Pallas kernels for 0%

profile of v12, /device:TPU:8, one launch (start us, length us, event | category | flops | bytes accessed | tf_op | source)
XLA Modules:
  0.0 142.5 jit_solution(4538851893115004101)
XLA Ops:
  0.0 1.2 shard_map.28
  1.2 18.4 %all_to_all.30 = bf16[16,2,80,128]{3,2,1,0:T(8,128)(2,1)S(1)} all-to-all(bf16[16,2,80,128]{3,2,1,0:T(8,128)(2,1)S(1)} %get-tuple-element.10), channel_id=1, replica_groups=mesh['chip'=8,'core'=2,'y'=8,'z'=4] {'chip','core'}, dimensions={0} | all-to-all | bytes 1310720 | tf_op jit(solution)/shard_map/all_to_all | solution.py:17
  19.5 37.1 %all_to_all.31 = bf16[32,80,128]{2,1,0:T(8,128)(2,1)S(1)} all-to-all(bf16[32,80,128]{2,1,0:T(8,128)(2,1)S(1)} %bitcast.16), channel_id=1, replica_groups=mesh['chip'=8,'core'=2,'y'=8,'z'=4] {'y','z'}, dimensions={0} | all-to-all | bytes 1310720 | tf_op jit(solution)/shard_map/all_to_all | solution.py:17
  56.6 0.1 slice.16
  56.8 0.1 broadcast_in_dim.21
  56.9 0.1 pad_maximum_fusion
  57.0 21.9 %all_to_all.32.own_ref = bf16[8,768,128]{2,1,0:T(8,128)(2,1)S(1)} all-to-all(bf16[8,768,128]{2,1,0:T(8,128)(2,1)S(1)} %pad_maximum_fusion), channel_id=1, replica_groups=mesh['chip'=8,'core'=2,'y'=8,'z'=4] {'chip'}, dimensions={0} | all-to-all | bytes 3145728 | tf_op jit(solution)/shard_map/all_to_all | solution.py:17
  79.0 0.3 constant_dynamic-slice_fusion
  79.3 1.9 %collective-permute-start = (bf16[8,640,128]{2,1,0:T(8,128)(2,1)S(1)}, bf16[8,640,128]{2,1,0:T(8,128)(2,1)S(1)}, u32[]{:S(2)}, u32[]{:S(2)}) collective-permute-start(bf16[8,640,128]{2,1,0:T(8,128)(2,1)S(1)} %constant_dynamic-slice_fusion), channel_id=1, source_target_pairs={{0,32},{32,0},{1,33},{33,1},{2,34},{34,2},{3,35},{35,3},{4,36},{36... | collective-permute-start | bytes 3932168 | tf_op jit(solution)/shard_map/ppermute | solution.py:160
  81.2 0.5 shard_map.29.early_ref
  81.7 2.5 %collective-permute-done.other_ref = bf16[8,640,128]{2,1,0:T(8,128)(2,1)S(1)} collective-permute-done((bf16[8,640,128]{2,1,0:T(8,128)(2,1)S(1)}, bf16[8,640,128]{2,1,0:T(8,128)(2,1)S(1)}, u32[]{:S(2)}, u32[]{:S(2)}) %collective-permute-start) | collective-permute-done | bytes 1310752 | tf_op jit(solution)/shard_map/ppermute | solution.py:160
  84.2 1.0 shard_map.30
  85.2 27.1 %all_to_all.33 = bf16[32,32,256]{2,1,0:T(8,128)(2,1)S(1)} all-to-all(bf16[32,32,256]{2,1,0:T(8,128)(2,1)S(1)} %bitcast.15), channel_id=1, replica_groups=mesh['chip'=8,'core'=2,'y'=8,'z'=4] {'z','y'}, dimensions={0} | all-to-all | bytes 1048576 | tf_op jit(solution)/shard_map/all_to_all | solution.py:17
  112.4 0.1 reduce_sum.12
  112.5 11.3 %all_to_all.34 = bf16[8,32,256]{2,1,0:T(8,128)(2,1)S(1)} all-to-all(bf16[8,32,256]{2,1,0:T(8,128)(2,1)S(1)} %broadcast_in_dim.22), channel_id=1, replica_groups=mesh['chip'=8,'core'=2,'y'=8,'z'=4] {'y'}, dimensions={0} | all-to-all | bytes 262144 | tf_op jit(solution)/shard_map/all_to_all | solution.py:17
  123.9 17.2 %all_to_all.35 = bf16[4,256,256]{2,1,0:T(8,128)(2,1)S(1)} all-to-all(bf16[4,256,256]{2,1,0:T(8,128)(2,1)S(1)} %broadcast_in_dim.24), channel_id=1, replica_groups=mesh['chip'=8,'core'=2,'y'=8,'z'=4] {'z'}, dimensions={0} | all-to-all | bytes 1048576 | tf_op jit(solution)/shard_map/all_to_all | solution.py:17
  141.0 1.5 %shard_map.31 = bf16[1,8,256,128]{3,2,1,0:T(8,128)(2,1)} custom-call(bf16[1024,256]{1,0:T(8,128)(2,1)S(1)} %bitcast.14, bf16[8,768,128]{2,1,0:T(8,128)(2,1)S(1)} %all_to_all.32.own_ref, bf16[8,640,128]{2,1,0:T(8,128)(2,1)S(1)} %collective-permute-done.other_ref), custom_call_target="tpu_custom_call" | custom-call | tf_op jit(solution)/shard_map/pallas_call | solution.py:119
  (4 shorter events, 0.1 us)
Async XLA Ops:
  79.3 4.9 %collective-permute-start = (bf16[8,640,128]{2,1,0:T(8,128)(2,1)S(1)}, bf16[8,640,128]{2,1,0:T(8,128)(2,1)S(1)}, u32[]{:S(2)}, u32[]{:S(2)}) collective-permute-start(bf16[8,640,128]{2,1,0:T(8,128)(2,1)S(1)} %constant_dynamic-slice_fusion), channel_id=1, source_target_pairs={{0,32},{32,0},{1,33},{33,1},{2,34},{34,2},{3,35},{35,3},{4,36},{36... | collective-permute-start | bytes 3932168 | tf_op jit(solution)/shard_map/ppermute | solution.py:160

commit v13 on v9

--- a/solution.py
+++ b/solution.py
@@ -160,10 +160,12 @@
     (early,) = call(early_kernel, [(aux // 2, block_a)], [own, kept], dtype=F32)
     (partial,) = call(fit_kernel, [(aux, block_a)], [own, other, kept, early])
 
-    parts = exchange(partial.reshape(cols, block_q, block_a), "col")
-    shard = jnp.sum(parts.astype(F32), axis=0).astype(BF16)
-    copies = jnp.broadcast_to(shard[None], (cols, block_q, block_a))
-    fitted = exchange(copies, "col").reshape(aux, block_a)
+    group = ("core", "col")
+    block = (block_q // cores, block_a)
+    parts = exchange(partial.reshape((cores * cols,) + block), group)
+    shards = jnp.sum(parts.reshape((cores, cols) + block).astype(F32), axis=1).astype(BF16)
+    copies = jnp.broadcast_to(shards[:, None], (cores, cols) + block)
+    fitted = exchange(copies.reshape((cores * cols,) + block), group).reshape(aux, block_a)
 
     (result,) = call(
         project_kernel,

time: 138 us -> 140 us (1.014)
  the two profiles are of different devices: /device:TPU:8 before, /device:TPU:1 now
where the time goes in v13:
time: 140 us
  blocking collectives  127 us (91%)
  starting transfers between devices  5.9 us (4%)
  Pallas kernels  4.13 us (3%)
  waiting for transfers between devices  2.16 us (2%)
    all_to_all x5, blocking collectives, exchange(): return lax.all_to_all(value, axes, 0, 0, tiled=True)  127 us
    ppermute x1, starting transfers between devices, body(): other = lax.ppermute(other, 'core', [(0, 1), (1, 0)])  5.9 us
    pallas_call x4, Pallas kernels, call(): pl.pallas_call(kernel, out_shape=[jax.ShapeDtypeStruct(shape, dtype) for...  4.13 us
  transfers between devices with their start and end apart: 1, of which 1 were waited for; matrix products, arithmetic and copies ran while one was open for 0% of the time, Pallas kernels for 0%

profile of v13, /device:TPU:1, one launch (start us, length us, event | category | flops | bytes accessed | tf_op | source)
XLA Modules:
  0.0 140.1 jit_solution(9649296613534698954)
XLA Ops:
  0.0 1.2 shard_map.28
  1.2 21.1 %all_to_all.25 = bf16[16,2,80,128]{3,2,1,0:T(8,128)(2,1)S(1)} all-to-all(bf16[16,2,80,128]{3,2,1,0:T(8,128)(2,1)S(1)} %get-tuple-element.10), channel_id=1, replica_groups=mesh['chip'=8,'core'=2,'col'=32] {'chip','core'}, dimensions={0} | all-to-all | bytes 1310720 | tf_op jit(solution)/shard_map/all_to_all | solution.py:16
  22.3 32.5 %all_to_all.26 = bf16[32,80,128]{2,1,0:T(8,128)(2,1)S(1)} all-to-all(bf16[32,80,128]{2,1,0:T(8,128)(2,1)S(1)} %bitcast.18), channel_id=1, replica_groups=mesh['chip'=8,'core'=2,'col'=32] {'col'}, dimensions={0} | all-to-all | bytes 1310720 | tf_op jit(solution)/shard_map/all_to_all | solution.py:16
  54.8 0.1 slice.16
  55.0 0.1 broadcast_in_dim.14
  55.1 0.1 pad_maximum_fusion
  55.2 20.8 %all_to_all.27.own_ref = bf16[8,768,128]{2,1,0:T(8,128)(2,1)S(1)} all-to-all(bf16[8,768,128]{2,1,0:T(8,128)(2,1)S(1)} %pad_maximum_fusion), channel_id=1, replica_groups=mesh['chip'=8,'core'=2,'col'=32] {'chip'}, dimensions={0} | all-to-all | bytes 3145728 | tf_op jit(solution)/shard_map/all_to_all | solution.py:16
  76.0 0.3 constant_dynamic-slice_fusion
  76.4 5.9 %collective-permute-start = (bf16[8,640,128]{2,1,0:T(8,128)(2,1)S(1)}, bf16[8,640,128]{2,1,0:T(8,128)(2,1)S(1)}, u32[]{:S(2)}, u32[]{:S(2)}) collective-permute-start(bf16[8,640,128]{2,1,0:T(8,128)(2,1)S(1)} %constant_dynamic-slice_fusion), channel_id=1, source_target_pairs={{0,32},{32,0},{1,33},{33,1},{2,34},{34,2},{3,35},{35,3},{4,36},{36... | collective-permute-start | bytes 3932168 | tf_op jit(solution)/shard_map/ppermute | solution.py:158
  82.3 0.5 shard_map.29.early_ref
  82.8 2.2 %collective-permute-done.other_ref = bf16[8,640,128]{2,1,0:T(8,128)(2,1)S(1)} collective-permute-done((bf16[8,640,128]{2,1,0:T(8,128)(2,1)S(1)}, bf16[8,640,128]{2,1,0:T(8,128)(2,1)S(1)}, u32[]{:S(2)}, u32[]{:S(2)}) %collective-permute-start) | collective-permute-done | bytes 1310752 | tf_op jit(solution)/shard_map/ppermute | solution.py:158
  84.9 1.0 shard_map.30
  86.0 27.3 %all_to_all.28 = bf16[64,16,256]{2,1,0:T(8,128)(2,1)S(1)} all-to-all(bf16[64,16,256]{2,1,0:T(8,128)(2,1)S(1)} %bitcast.17), channel_id=1, replica_groups=mesh['chip'=8,'core'=2,'col'=32] {'core','col'}, dimensions={0} | all-to-all | bytes 1048576 | tf_op jit(solution)/shard_map/all_to_all | solution.py:16
  113.3 0.1 bitcast_reduce_fusion
  113.4 25.2 %all_to_all.29 = bf16[64,16,256]{2,1,0:T(8,128)(2,1)S(1)} all-to-all(bf16[64,16,256]{2,1,0:T(8,128)(2,1)S(1)} %bitcast.20), channel_id=1, replica_groups=mesh['chip'=8,'core'=2,'col'=32] {'core','col'}, dimensions={0} | all-to-all | bytes 1048576 | tf_op jit(solution)/shard_map/all_to_all | solution.py:16
  138.6 1.5 %shard_map.31 = bf16[1,8,256,128]{3,2,1,0:T(8,128)(2,1)} custom-call(bf16[1024,256]{1,0:T(8,128)(2,1)S(1)} %bitcast.16, bf16[8,768,128]{2,1,0:T(8,128)(2,1)S(1)} %all_to_all.27.own_ref, bf16[8,640,128]{2,1,0:T(8,128)(2,1)S(1)} %collective-permute-done.other_ref), custom_call_target="tpu_custom_call" | custom-call | tf_op jit(solution)/shard_map/pallas_call | solution.py:118
  (3 shorter events, 0.1 us)
Async XLA Ops:
  76.4 8.6 %collective-permute-start = (bf16[8,640,128]{2,1,0:T(8,128)(2,1)S(1)}, bf16[8,640,128]{2,1,0:T(8,128)(2,1)S(1)}, u32[]{:S(2)}, u32[]{:S(2)}) collective-permute-start(bf16[8,640,128]{2,1,0:T(8,128)(2,1)S(1)} %constant_dynamic-slice_fusion), channel_id=1, source_target_pairs={{0,32},{32,0},{1,33},{33,1},{2,34},{34,2},{3,35},{35,3},{4,36},{36... | collective-permute-start | bytes 3932168 | tf_op jit(solution)/shard_map/ppermute | solution.py:158

commit v14 on v8

--- a/solution.py
+++ b/solution.py
@@ -16,37 +16,38 @@
     return lax.all_to_all(value, axes, 0, 0, tiled=True)
 
 
-def places(core, block_b, aux_half):
-    own_t = pl.multiple_of(core * (block_b + aux_half), block_b)
-    other_t = pl.multiple_of(core * aux_half, block_b)
-    other_f = pl.multiple_of((1 - core) * block_b, block_b)
-    return own_t, other_t, other_f
-
-
-def fit_kernel(own_ref, other_ref, t_ref, out_ref):
-    _, nj, block_a, block_b = t_ref.shape
+def product(held_ref, first, count, own_ref, other_ref, t_ref):
+    _, nj, _, block_b = t_ref.shape
     half = block_b // 2
-    aux_half = out_ref.shape[0] // 2
     core = lax.axis_index("core")
-    own_t, other_t, other_f = places(core, block_b, aux_half)
-    straight = jnp.concatenate([t_ref[0, j] for j in range(nj)], axis=1)
+    own_t = pl.multiple_of(core * (own_ref.shape[1] - block_b), block_b)
     columns = []
     for side in range(2):
         blocks = []
         for j in range(nj):
             mine = own_ref[j, pl.ds(own_t + side * half, half), :]
-            theirs = other_ref[j, pl.ds(other_t + side * half, half), :]
+            theirs = other_ref[j, pl.ds(side * half, half), :]
             blocks.append(jnp.where(core == 0, mine, theirs))
             blocks.append(jnp.where(core == 0, theirs, mine))
         columns.append(jnp.concatenate(blocks, axis=0))
     swapped = jnp.concatenate(columns, axis=1)
-    for s, (ref, start) in enumerate(((own_ref, block_b), (other_ref, other_f))):
-        held = jnp.concatenate([ref[j, pl.ds(start, aux_half), :] for j in range(nj)], axis=1)
-        direct = lax.dot_general(
-            held, straight, (((1,), (1,)), ((), ())), preferred_element_type=F32
-        )
-        mirror = jnp.dot(held, swapped, preferred_element_type=F32)
-        out_ref[pl.ds(s * aux_half, aux_half), :] = (2.0 * direct - mirror).astype(BF16)
+    straight = jnp.concatenate([t_ref[0, j] for j in range(nj)], axis=1)
+    held = jnp.concatenate([held_ref[j, pl.ds(first, count), :] for j in range(nj)], axis=1)
+    direct = lax.dot_general(
+        held, straight, (((1,), (1,)), ((), ())), preferred_element_type=F32
+    )
+    mirror = jnp.dot(held, swapped, preferred_element_type=F32)
+    return (2.0 * direct - mirror).astype(BF16)
+
+
+def early_kernel(own_ref, other_ref, t_ref, out_ref):
+    out_ref[...] = product(own_ref, t_ref.shape[3], out_ref.shape[0], own_ref, other_ref, t_ref)
+
+
+def late_kernel(own_ref, other_ref, factors_ref, t_ref, early_ref, out_ref):
+    count = early_ref.shape[0]
+    out_ref[pl.ds(0, count), :] = early_ref[...]
+    out_ref[pl.ds(count, count), :] = product(factors_ref, 0, count, own_ref, other_ref, t_ref)
 
 
 def pack_kernel(t_hbm, f_hbm, out_ref, t_ref, f_ref, sems):
@@ -75,7 +76,6 @@
 def project_kernel(fitted_ref, own_ref, other_ref, out_hbm, out_ref, sems):
     _, nj, _, block_b = out_ref.shape
     aux_half = fitted_ref.shape[0] // 2
-    _, _, other_f = places(lax.axis_index("core"), block_b, aux_half)
     turned = fitted_ref[...].T
     stores = []
     for j in range(0, nj, 2):
@@ -84,7 +84,7 @@
                 jnp.concatenate(
                     [
                         own_ref[j + i, pl.ds(block_b, aux_half), :],
-                        other_ref[j + i, pl.ds(other_f, aux_half), :],
+                        other_ref[j + i],
                     ],
                     axis=0,
                 )
@@ -131,7 +131,7 @@
         inside=HBM,
         scratch=[pltpu.VMEM(factors.shape, BF16), pltpu.SemaphoreType.DMA((2,))],
     )
-    start = ((1 - lax.axis_index("core")) * block_b).astype(jnp.uint32)
+    start = ((1 - lax.axis_index("core")) * (block_b + aux // 2)).astype(jnp.uint32)
     both, start = lax.optimization_barrier((both, start))
     both = exchange(both, ROW)
     both = exchange(both.reshape(cols, half + few, block_b), "col")
@@ -142,10 +142,13 @@
     own = exchange(jnp.concatenate([x[:, 0], y, x[:, 1]], axis=1), "chip")
 
     zero = jnp.uint32(0)
-    other = lax.dynamic_slice(own, (zero, start, zero), (chips, block_b + aux // 2, block_b))
-    other = lax.ppermute(other, "core", [(0, 1), (1, 0)])
+    swap = [(0, 1), (1, 0)]
+    sent = lax.dynamic_slice(own, (zero, start, zero), (chips, block_b, block_b))
+    turned = lax.ppermute(sent, "core", swap)
+    other = lax.ppermute(own[:, block_b : block_b + aux // 2], "core", swap)
 
-    (partial,) = call(fit_kernel, [(aux, block_a)], [own, other, kept])
+    (early,) = call(early_kernel, [(aux // 2, block_a)], [own, turned, kept])
+    (partial,) = call(late_kernel, [(aux, block_a)], [own, turned, other, kept, early])
 
     parts = exchange(partial.reshape(cols, block_q, block_a), "col")
     shard = jnp.sum(parts.astype(F32), axis=0).astype(BF16)

time: 138 us -> 139 us (level)
  starting transfers between devices: 1.92 us -> 4.33 us
  waiting for transfers between devices: 3 us -> 1.14 us
    ppermute x1 -> x2, starting transfers between devices: 1.92 us -> 4.33 us  [the longest x1 2.41 us: body(): turned = lax.ppermute(sent, 'core', swap)]
    ppermute x1 -> x2, waiting for transfers between devices: 3 us -> 1.14 us  [the longest x1 1.14 us: body(): turned = lax.ppermute(sent, 'core', swap)]
    pallas_call x3 -> x4, Pallas kernels: 3.94 us -> 4.12 us  [call(): pl.pallas_call(kernel, out_shape=[jax.ShapeDtypeStruct(shape, BF16) for s...]
  transfers between devices with their start and end apart: 1 -> 2, of which waited for: 1 -> 1; matrix products, arithmetic and copies ran while one was open for 0% -> 0% of each run, Pallas kernels for 0% -> 1%
where the time goes in v14:
time: 139 us; the launch traced here: 138 us
  blocking collectives  128 us (92%)
  starting transfers between devices  4.33 us (3%)
  Pallas kernels  4.12 us (3%)
    all_to_all x5, blocking collectives, exchange(): return lax.all_to_all(value, axes, 0, 0, tiled=True)  128 us
    pallas_call x4, Pallas kernels, call(): pl.pallas_call(kernel, out_shape=[jax.ShapeDtypeStruct(shape, BF16) for s...  4.12 us
  transfers between devices with their start and end apart: 2, of which 1 were waited for; matrix products, arithmetic and copies ran while one was open for 0% of the time, Pallas kernels for 1%

profile of v14, /device:TPU:8, one launch (start us, length us, event | category | flops | bytes accessed | tf_op | source)
XLA Modules:
  0.0 138.5 jit_solution(8952872243918300705)
XLA Ops:
  0.0 1.2 shard_map.28
  1.2 18.4 %all_to_all.25 = bf16[16,2,80,128]{3,2,1,0:T(8,128)(2,1)S(1)} all-to-all(bf16[16,2,80,128]{3,2,1,0:T(8,128)(2,1)S(1)} %get-tuple-element.10), channel_id=1, replica_groups=mesh['chip'=8,'core'=2,'col'=32] {'chip','core'}, dimensions={0} | all-to-all | bytes 1310720 | tf_op jit(solution)/shard_map/all_to_all | solution.py:16
  19.5 37.1 %all_to_all.26 = bf16[32,80,128]{2,1,0:T(8,128)(2,1)S(1)} all-to-all(bf16[32,80,128]{2,1,0:T(8,128)(2,1)S(1)} %bitcast.15), channel_id=1, replica_groups=mesh['chip'=8,'core'=2,'col'=32] {'col'}, dimensions={0} | all-to-all | bytes 1310720 | tf_op jit(solution)/shard_map/all_to_all | solution.py:16
  56.6 0.1 slice.20
  56.8 0.1 broadcast_in_dim.14
  56.9 0.1 pad_maximum_fusion
  57.0 21.9 %all_to_all.27.own_ref = bf16[8,768,128]{2,1,0:T(8,128)(2,1)S(1)} all-to-all(bf16[8,768,128]{2,1,0:T(8,128)(2,1)S(1)} %pad_maximum_fusion), channel_id=1, replica_groups=mesh['chip'=8,'core'=2,'col'=32] {'chip'}, dimensions={0} | all-to-all | bytes 3145728 | tf_op jit(solution)/shard_map/all_to_all | solution.py:16
  79.0 0.1 slice.24
  79.0 1.9 %collective-permute-start.1 = (bf16[8,512,128]{2,1,0:T(8,128)(2,1)S(1)}, bf16[8,512,128]{2,1,0:T(8,128)(2,1)S(1)}, u32[]{:S(2)}, u32[]{:S(2)}) collective-permute-start(bf16[8,512,128]{2,1,0:T(8,128)(2,1)S(1)} %slice.24), channel_id=1, source_target_pairs={{0,32},{32,0},{1,33},{33,1},{2,34},{34,2},{3,35},{35,3},{4,36},{36... | collective-permute-start | bytes 3145736 | tf_op jit(solution)/shard_map/ppermute | solution.py:148
  81.0 0.1 constant_dynamic-slice_fusion
  81.1 2.4 %collective-permute-start = (bf16[8,128,128]{2,1,0:T(8,128)(2,1)S(1)}, bf16[8,128,128]{2,1,0:T(8,128)(2,1)S(1)}, u32[]{:S(2)}, u32[]{:S(2)}) collective-permute-start(bf16[8,128,128]{2,1,0:T(8,128)(2,1)S(1)} %constant_dynamic-slice_fusion), channel_id=1, source_target_pairs={{0,32},{32,0},{1,33},{33,1},{2,34},{34,2},{3,35},{35,3},{4,36},{36... | collective-permute-start | bytes 786440 | tf_op jit(solution)/shard_map/ppermute | solution.py:147
  83.5 1.1 collective-permute-done.other_ref
  84.6 0.7 shard_map.29.early_ref
  85.3 0.0 collective-permute-done.1.factors_ref.other_ref
  85.4 0.7 shard_map.30
  86.1 26.7 %all_to_all.28 = bf16[32,32,256]{2,1,0:T(8,128)(2,1)S(1)} all-to-all(bf16[32,32,256]{2,1,0:T(8,128)(2,1)S(1)} %bitcast.14), channel_id=1, replica_groups=mesh['chip'=8,'core'=2,'col'=32] {'col'}, dimensions={0} | all-to-all | bytes 1048576 | tf_op jit(solution)/shard_map/all_to_all | solution.py:16
  112.7 0.1 reduce_sum.12
  112.8 0.1 broadcast_in_dim.15
  112.9 24.1 %all_to_all.29 = bf16[32,32,256]{2,1,0:T(8,128)(2,1)S(1)} all-to-all(bf16[32,32,256]{2,1,0:T(8,128)(2,1)S(1)} %broadcast_in_dim.15), channel_id=1, replica_groups=mesh['chip'=8,'core'=2,'col'=32] {'col'}, dimensions={0} | all-to-all | bytes 1048576 | tf_op jit(solution)/shard_map/all_to_all | solution.py:16
  137.0 1.5 %shard_map.31 = bf16[1,8,256,128]{3,2,1,0:T(8,128)(2,1)} custom-call(bf16[1024,256]{1,0:T(8,128)(2,1)S(1)} %bitcast.13, bf16[8,768,128]{2,1,0:T(8,128)(2,1)S(1)} %all_to_all.27.own_ref, bf16[8,512,128]{2,1,0:T(8,128)(2,1)S(1)} %collective-permute-done.1.factors_ref.other_ref), custom_call_target="tpu_custom_call" | custom-call | tf_op jit(solution)/shard_map/pallas_call | solution.py:106
  (2 shorter events, 0.0 us)
Async XLA Ops:
  79.0 6.3 %collective-permute-start.1 = (bf16[8,512,128]{2,1,0:T(8,128)(2,1)S(1)}, bf16[8,512,128]{2,1,0:T(8,128)(2,1)S(1)}, u32[]{:S(2)}, u32[]{:S(2)}) collective-permute-start(bf16[8,512,128]{2,1,0:T(8,128)(2,1)S(1)} %slice.24), channel_id=1, source_target_pairs={{0,32},{32,0},{1,33},{33,1},{2,34},{34,2},{3,35},{35,3},{4,36},{36... | collective-permute-start | bytes 3145736 | tf_op jit(solution)/shard_map/ppermute | solution.py:148
  81.1 3.6 %collective-permute-start = (bf16[8,128,128]{2,1,0:T(8,128)(2,1)S(1)}, bf16[8,128,128]{2,1,0:T(8,128)(2,1)S(1)}, u32[]{:S(2)}, u32[]{:S(2)}) collective-permute-start(bf16[8,128,128]{2,1,0:T(8,128)(2,1)S(1)} %constant_dynamic-slice_fusion), channel_id=1, source_target_pairs={{0,32},{32,0},{1,33},{33,1},{2,34},{34,2},{3,35},{35,3},{4,36},{36... | collective-permute-start | bytes 786440 | tf_op jit(solution)/shard_map/ppermute | solution.py:147

commit v15 on v9

--- a/solution.py
+++ b/solution.py
@@ -84,6 +84,11 @@
                 out_ref[2 * j + bit, side, pl.ds(0, half), :] = t_ref[0, j, rows, :]
 
 
+def sum_kernel(parts_ref, out_ref):
+    total = jnp.sum(parts_ref[...].astype(F32), axis=0).astype(BF16)
+    out_ref[...] = jnp.broadcast_to(total[None], out_ref.shape)
+
+
 def project_kernel(fitted_ref, own_ref, other_ref, out_hbm, out_ref, sems):
     _, nj, _, block_b = out_ref.shape
     aux_half = fitted_ref.shape[0] // 2
@@ -161,8 +166,7 @@
     (partial,) = call(fit_kernel, [(aux, block_a)], [own, other, kept, early])
 
     parts = exchange(partial.reshape(cols, block_q, block_a), "col")
-    shard = jnp.sum(parts.astype(F32), axis=0).astype(BF16)
-    copies = jnp.broadcast_to(shard[None], (cols, block_q, block_a))
+    (copies,) = call(sum_kernel, [parts.shape], [parts])
     fitted = exchange(copies, "col").reshape(aux, block_a)
 
     (result,) = call(

time: 138 us -> 138 us (level)
    pallas_call x4 -> x5, Pallas kernels: 4.13 us -> 4.23 us  [call(): pl.pallas_call(kernel, out_shape=[jax.ShapeDtypeStruct(shape, dtype) for...]
where the time goes in v15:
time: 138 us; the launch traced here: 137 us
  blocking collectives  128 us (93%)
  Pallas kernels  4.23 us (3%)
  waiting for transfers between devices  2.52 us (2%)
  starting transfers between devices  1.92 us (1%)
    all_to_all x5, blocking collectives, exchange(): return lax.all_to_all(value, axes, 0, 0, tiled=True)  128 us
    pallas_call x5, Pallas kernels, call(): pl.pallas_call(kernel, out_shape=[jax.ShapeDtypeStruct(shape, dtype) for...  4.23 us
  transfers between devices with their start and end apart: 1, of which 1 were waited for; matrix products, arithmetic and copies ran while one was open for 0% of the time, Pallas kernels for 0%

profile of v15, /device:TPU:8, one launch (start us, length us, event | category | flops | bytes accessed | tf_op | source)
XLA Modules:
  0.0 137.3 jit_solution(1735828162353043499)
XLA Ops:
  0.0 1.2 shard_map.28
  1.2 18.4 %all_to_all.25 = bf16[16,2,80,128]{3,2,1,0:T(8,128)(2,1)S(1)} all-to-all(bf16[16,2,80,128]{3,2,1,0:T(8,128)(2,1)S(1)} %get-tuple-element.10), channel_id=1, replica_groups=mesh['chip'=8,'core'=2,'col'=32] {'chip','core'}, dimensions={0} | all-to-all | bytes 1310720 | tf_op jit(solution)/shard_map/all_to_all | solution.py:16
  19.5 37.1 %all_to_all.26 = bf16[32,80,128]{2,1,0:T(8,128)(2,1)S(1)} all-to-all(bf16[32,80,128]{2,1,0:T(8,128)(2,1)S(1)} %bitcast.15), channel_id=1, replica_groups=mesh['chip'=8,'core'=2,'col'=32] {'col'}, dimensions={0} | all-to-all | bytes 1310720 | tf_op jit(solution)/shard_map/all_to_all | solution.py:16
  56.6 0.1 slice.16
  56.8 0.1 broadcast_in_dim.8
  56.9 0.1 pad_maximum_fusion
  57.0 21.9 %all_to_all.27.own_ref = bf16[8,768,128]{2,1,0:T(8,128)(2,1)S(1)} all-to-all(bf16[8,768,128]{2,1,0:T(8,128)(2,1)S(1)} %pad_maximum_fusion), channel_id=1, replica_groups=mesh['chip'=8,'core'=2,'col'=32] {'chip'}, dimensions={0} | all-to-all | bytes 3145728 | tf_op jit(solution)/shard_map/all_to_all | solution.py:16
  79.0 0.3 constant_dynamic-slice_fusion
  79.3 1.9 %collective-permute-start = (bf16[8,640,128]{2,1,0:T(8,128)(2,1)S(1)}, bf16[8,640,128]{2,1,0:T(8,128)(2,1)S(1)}, u32[]{:S(2)}, u32[]{:S(2)}) collective-permute-start(bf16[8,640,128]{2,1,0:T(8,128)(2,1)S(1)} %constant_dynamic-slice_fusion), channel_id=1, source_target_pairs={{0,32},{32,0},{1,33},{33,1},{2,34},{34,2},{3,35},{35,3},{4,36},{36... | collective-permute-start | bytes 3932168 | tf_op jit(solution)/shard_map/ppermute | solution.py:163
  81.2 0.5 shard_map.29.early_ref
  81.7 2.5 %collective-permute-done.other_ref = bf16[8,640,128]{2,1,0:T(8,128)(2,1)S(1)} collective-permute-done((bf16[8,640,128]{2,1,0:T(8,128)(2,1)S(1)}, bf16[8,640,128]{2,1,0:T(8,128)(2,1)S(1)}, u32[]{:S(2)}, u32[]{:S(2)}) %collective-permute-start) | collective-permute-done | bytes 1310752 | tf_op jit(solution)/shard_map/ppermute | solution.py:163
  84.2 1.0 shard_map.30
  85.2 26.4 %all_to_all.28.parts_ref = bf16[32,32,256]{2,1,0:T(8,128)(2,1)S(1)} all-to-all(bf16[32,32,256]{2,1,0:T(8,128)(2,1)S(1)} %bitcast.14), channel_id=1, replica_groups=mesh['chip'=8,'core'=2,'col'=32] {'col'}, dimensions={0} | all-to-all | bytes 1048576 | tf_op jit(solution)/shard_map/all_to_all | solution.py:16
  111.7 0.1 shard_map.31
  111.8 24.0 %all_to_all.29 = bf16[32,32,256]{2,1,0:T(8,128)(2,1)S(1)} all-to-all(bf16[32,32,256]{2,1,0:T(8,128)(2,1)S(1)} %shard_map.31), channel_id=1, replica_groups=mesh['chip'=8,'core'=2,'col'=32] {'col'}, dimensions={0} | all-to-all | bytes 1048576 | tf_op jit(solution)/shard_map/all_to_all | solution.py:16
  135.8 1.5 %shard_map.32 = bf16[1,8,256,128]{3,2,1,0:T(8,128)(2,1)} custom-call(bf16[1024,256]{1,0:T(8,128)(2,1)S(1)} %bitcast.13, bf16[8,768,128]{2,1,0:T(8,128)(2,1)S(1)} %all_to_all.27.own_ref, bf16[8,640,128]{2,1,0:T(8,128)(2,1)S(1)} %collective-permute-done.other_ref), custom_call_target="tpu_custom_call" | custom-call | tf_op jit(solution)/shard_map/pallas_call | solution.py:123
  (2 shorter events, 0.0 us)
Async XLA Ops:
  79.3 4.9 %collective-permute-start = (bf16[8,640,128]{2,1,0:T(8,128)(2,1)S(1)}, bf16[8,640,128]{2,1,0:T(8,128)(2,1)S(1)}, u32[]{:S(2)}, u32[]{:S(2)}) collective-permute-start(bf16[8,640,128]{2,1,0:T(8,128)(2,1)S(1)} %constant_dynamic-slice_fusion), channel_id=1, source_target_pairs={{0,32},{32,0},{1,33},{33,1},{2,34},{34,2},{3,35},{35,3},{4,36},{36... | collective-permute-start | bytes 3932168 | tf_op jit(solution)/shard_map/ppermute | solution.py:163

commit v16 on v11

--- a/solution.py
+++ b/solution.py
@@ -98,11 +98,6 @@
             out_ref[chip, pl.ds(place, half), :] = both_ref[chip * per_chip + i, pl.ds(0, half), :]
 
 
-def sum_kernel(parts_ref, out_ref):
-    total = jnp.sum(parts_ref[...].astype(F32), axis=0).astype(BF16)
-    out_ref[...] = jnp.broadcast_to(total[None], out_ref.shape)
-
-
 def project_kernel(fitted_ref, own_ref, other_ref, out_hbm, out_ref, sems):
     _, nj, _, block_b = out_ref.shape
     aux_half = fitted_ref.shape[0] // 2
@@ -178,7 +173,8 @@
     (partial,) = call(fit_kernel, [(aux, block_a)], [own, other, kept, early])
 
     parts = exchange(partial.reshape(cols, block_q, block_a), "col")
-    (copies,) = call(sum_kernel, [parts.shape], [parts])
+    shard = jnp.sum(parts.astype(F32), axis=0).astype(BF16)
+    copies = jnp.broadcast_to(shard[None], (cols, block_q, block_a))
     fitted = exchange(copies, "col").reshape(aux, block_a)
 
     (result,) = call(

time: 137 us -> 137 us (level)
    pallas_call x6 -> x5, Pallas kernels: 4.41 us -> 4.31 us  [call(): pl.pallas_call(kernel, out_shape=[jax.ShapeDtypeStruct(shape, dtype) for...]
where the time goes in v16:
time: 137 us
  blocking collectives  128 us (93%)
  Pallas kernels  4.31 us (3%)
  waiting for transfers between devices  2.52 us (2%)
  starting transfers between devices  1.92 us (1%)
    all_to_all x5, blocking collectives, exchange(): return lax.all_to_all(value, axes, 0, 0, tiled=True)  128 us
    pallas_call x5, Pallas kernels, call(): pl.pallas_call(kernel, out_shape=[jax.ShapeDtypeStruct(shape, dtype) for...  4.31 us
  transfers between devices with their start and end apart: 1, of which 1 were waited for; matrix products, arithmetic and copies ran while one was open for 0% of the time, Pallas kernels for 0%

profile of v16, /device:TPU:8, one launch (start us, length us, event | category | flops | bytes accessed | tf_op | source)
XLA Modules:
  0.0 137.1 jit_solution(3967419622910760904)
XLA Ops:
  0.0 1.2 shard_map.28
  1.2 18.4 %all_to_all.25 = bf16[16,2,80,128]{3,2,1,0:T(8,128)(2,1)S(1)} all-to-all(bf16[16,2,80,128]{3,2,1,0:T(8,128)(2,1)S(1)} %get-tuple-element.10), channel_id=1, replica_groups=mesh['chip'=8,'core'=2,'col'=32] {'chip','core'}, dimensions={0} | all-to-all | bytes 1310720 | tf_op jit(solution)/shard_map/all_to_all | solution.py:16
  19.5 37.1 %all_to_all.26.both_ref = bf16[32,80,128]{2,1,0:T(8,128)(2,1)S(1)} all-to-all(bf16[32,80,128]{2,1,0:T(8,128)(2,1)S(1)} %bitcast.5), channel_id=1, replica_groups=mesh['chip'=8,'core'=2,'col'=32] {'col'}, dimensions={0} | all-to-all | bytes 1310720 | tf_op jit(solution)/shard_map/all_to_all | solution.py:16
  56.6 0.2 shard_map.29
  56.8 21.9 %all_to_all.27.own_ref = bf16[8,768,128]{2,1,0:T(8,128)(2,1)S(1)} all-to-all(bf16[8,768,128]{2,1,0:T(8,128)(2,1)S(1)} %shard_map.29), channel_id=1, replica_groups=mesh['chip'=8,'core'=2,'col'=32] {'chip'}, dimensions={0} | all-to-all | bytes 3145728 | tf_op jit(solution)/shard_map/all_to_all | solution.py:16
  78.8 0.3 constant_dynamic-slice_fusion
  79.1 1.9 %collective-permute-start = (bf16[8,640,128]{2,1,0:T(8,128)(2,1)S(1)}, bf16[8,640,128]{2,1,0:T(8,128)(2,1)S(1)}, u32[]{:S(2)}, u32[]{:S(2)}) collective-permute-start(bf16[8,640,128]{2,1,0:T(8,128)(2,1)S(1)} %constant_dynamic-slice_fusion), channel_id=1, source_target_pairs={{0,32},{32,0},{1,33},{33,1},{2,34},{34,2},{3,35},{35,3},{4,36},{36... | collective-permute-start | bytes 3932168 | tf_op jit(solution)/shard_map/ppermute | solution.py:170
  81.0 0.5 shard_map.30.early_ref
  81.5 2.5 %collective-permute-done.other_ref = bf16[8,640,128]{2,1,0:T(8,128)(2,1)S(1)} collective-permute-done((bf16[8,640,128]{2,1,0:T(8,128)(2,1)S(1)}, bf16[8,640,128]{2,1,0:T(8,128)(2,1)S(1)}, u32[]{:S(2)}, u32[]{:S(2)}) %collective-permute-start) | collective-permute-done | bytes 1310752 | tf_op jit(solution)/shard_map/ppermute | solution.py:170
  84.0 1.0 shard_map.31
  85.0 26.4 %all_to_all.28 = bf16[32,32,256]{2,1,0:T(8,128)(2,1)S(1)} all-to-all(bf16[32,32,256]{2,1,0:T(8,128)(2,1)S(1)} %bitcast.4), channel_id=1, replica_groups=mesh['chip'=8,'core'=2,'col'=32] {'col'}, dimensions={0} | all-to-all | bytes 1048576 | tf_op jit(solution)/shard_map/all_to_all | solution.py:16
  111.5 0.1 reduce_sum.12
  111.6 0.1 broadcast_in_dim.2
  111.6 24.0 %all_to_all.29 = bf16[32,32,256]{2,1,0:T(8,128)(2,1)S(1)} all-to-all(bf16[32,32,256]{2,1,0:T(8,128)(2,1)S(1)} %broadcast_in_dim.2), channel_id=1, replica_groups=mesh['chip'=8,'core'=2,'col'=32] {'col'}, dimensions={0} | all-to-all | bytes 1048576 | tf_op jit(solution)/shard_map/all_to_all | solution.py:16
  135.6 1.5 %shard_map.32 = bf16[1,8,256,128]{3,2,1,0:T(8,128)(2,1)} custom-call(bf16[1024,256]{1,0:T(8,128)(2,1)S(1)} %bitcast.3, bf16[8,768,128]{2,1,0:T(8,128)(2,1)S(1)} %all_to_all.27.own_ref, bf16[8,640,128]{2,1,0:T(8,128)(2,1)S(1)} %collective-permute-done.other_ref), custom_call_target="tpu_custom_call" | custom-call | tf_op jit(solution)/shard_map/pallas_call | solution.py:132
Async XLA Ops:
  79.1 4.9 %collective-permute-start = (bf16[8,640,128]{2,1,0:T(8,128)(2,1)S(1)}, bf16[8,640,128]{2,1,0:T(8,128)(2,1)S(1)}, u32[]{:S(2)}, u32[]{:S(2)}) collective-permute-start(bf16[8,640,128]{2,1,0:T(8,128)(2,1)S(1)} %constant_dynamic-slice_fusion), channel_id=1, source_target_pairs={{0,32},{32,0},{1,33},{33,1},{2,34},{34,2},{3,35},{35,3},{4,36},{36... | collective-permute-start | bytes 3932168 | tf_op jit(solution)/shard_map/ppermute | solution.py:170
